TPU v7x, 128 devices: a whole 4x4x4 slice. The times are simulated.
128 devices in a mesh: lat: 8 (over y, core), lon: 16 (over z, x).
Axes of the slice: x: 4, y: 4, z: 4, core: 2. Of those that a mesh axis runs over, the one named last changes fastest.
Arguments:
- temp: float32 [64, 256, 2048], P(None, 'lat', 'lon'), may hold values from -6 to 6
- salt: float32 [64, 256, 2048], P(None, 'lat', 'lon'), may hold values from -6 to 6
- u_east: float32 [64, 256, 2048], P(None, 'lat', 'lon'), may hold values from -1.2 to 1.2
- v_north: float32 [64, 256, 2048], P(None, 'lat', 'lon'), may hold values from -1.2 to 1.2
- vdiff: float32 [64, 256, 2048], P(None, 'lat', 'lon'), may hold values from 0.05 to 5
- kmt: int32 [256, 2048], P('lat', 'lon'), may hold values from 0 to 64
- owner: int32 [4, 256, 2048], P(None, 'lat', 'lon'), may hold values from 0 to 127, as said below
- atmo_cell: int32 [4, 256, 2048], P(None, 'lat', 'lon'), may hold values from 0 to 2047
- weight: float32 [4, 256, 2048], P(None, 'lat', 'lon'), may hold values from 0.01 to 0.06
Outputs:
- temp_out: float32 [64, 256, 2048], P(None, 'lat', 'lon')
- salt_out: float32 [64, 256, 2048], P(None, 'lat', 'lon')
- atmo_fields: float32 [2, 262144], P(None, ('lat', 'lon'))
Inputs may be any that keep to these rules, and one draw needn't show every extreme that they name: Within each device's block of 32 x 128 ocean cells (all 4 links of a cell together) no owner is named by more than 512 links; in every draw one owner is named by exactly 512 links of every device's block.
All inputs are finite; a program needn't handle non-finite values.
Results may differ from a plain program's by a relative error of at most 0.00011.
Values sent between devices are 32-bit elements; how exact they have to be, the bound alone decides.
A program may use at most 128 MiB of HBM per device.

v0:
```python
import functools

import jax
import jax.numpy as jnp
from jax import lax
from jax.experimental import pallas as pl
from jax.experimental.pallas import tpu as pltpu
from jax.sharding import PartitionSpec as P


I32 = jnp.int32
F32 = jnp.float32


def lanes_of(x, idx):
    return jnp.take_along_axis(x, idx, axis=1, mode="promise_in_bounds")


def subs_of(x, idx):
    return jnp.take_along_axis(x, idx, axis=0, mode="promise_in_bounds")


def sort_links(keys, loads):
    lane = lax.broadcasted_iota(I32, (8, 128), 1)
    sub = lax.broadcasted_iota(I32, (8, 128), 0)
    lane_swap = [lane ^ (1 << b) for b in range(7)]
    sub_swap = [sub ^ (1 << b) for b in range(3)]

    def bit(b):
        if b < 4:
            return None
        if b < 7:
            return ((sub >> (b - 4)) & 1) == 1
        if b < 14:
            return ((lane >> (b - 7)) & 1) == 1
        return None

    for top in range(1, 15):
        for b in range(top - 1, -1, -1):
            down = bit(top)
            if b < 4:
                new_k, new_w = list(keys), list(loads)
                for v in range(16):
                    if (v >> b) & 1:
                        continue
                    u = v | (1 << b)
                    swap = keys[v] > keys[u]
                    if top < 4:
                        if (v >> top) & 1:
                            swap = keys[v] < keys[u]
                    elif down is not None:
                        swap = jnp.logical_xor(swap, down)
                    new_k[v] = jnp.where(swap, keys[u], keys[v])
                    new_k[u] = jnp.where(swap, keys[v], keys[u])
                    new_w[v] = jnp.where(swap, loads[u], loads[v])
                    new_w[u] = jnp.where(swap, loads[v], loads[u])
                keys, loads = new_k, new_w
            else:
                high = bit(b)
                keep_max = high if down is None else jnp.logical_xor(high, down)
                if b < 7:
                    fetch = functools.partial(subs_of, idx=sub_swap[b - 4])
                else:
                    fetch = functools.partial(lanes_of, idx=lane_swap[b - 7])
                new_k, new_w = [], []
                for v in range(16):
                    k, w = keys[v], loads[v]
                    pk, pw = fetch(k), fetch(w)
                    more, less = pk > k, pk < k
                    take = jnp.logical_or(
                        jnp.logical_and(keep_max, more),
                        jnp.logical_and(jnp.logical_not(keep_max), less),
                    )
                    new_k.append(jnp.where(take, pk, k))
                    new_w.append(jnp.where(take, pw, w))
                keys, loads = new_k, new_w
    return keys, loads


def owner_starts(keys):
    lane = lax.broadcasted_iota(I32, (8, 128), 1)
    first = jnp.broadcast_to(keys[0][0:1, :], (8, 128))
    bound = lane << 23
    count = jnp.zeros((8, 128), I32)
    for step in (128, 64, 32, 16, 8, 4, 2, 1):
        trial = count + step
        value = lanes_of(first, jnp.minimum(trial - 1, 127))
        fits = jnp.logical_and(trial <= 128, value < bound)
        count = jnp.where(fits, trial, count)
    column = jnp.maximum(count - 1, 0)
    within = jnp.zeros((8, 128), I32)
    for v in range(16):
        within = within + jnp.where(lanes_of(keys[v], column) < bound, 1, 0)
    within = jnp.broadcast_to(jnp.sum(within, axis=0, keepdims=True), (8, 128))
    return jnp.where(count > 0, column * 128 + within, 0)


def owner_slots(tiles, start):
    sub = lax.broadcasted_iota(I32, (8, 128), 0)
    column = start >> 7
    turn = start & 127
    x = []
    for c in range(5):
        idx = jnp.minimum(column + c, 127)
        x.append([lanes_of(tiles[v], idx) for v in range(16)])
    for n in (64, 32, 16):
        on = (turn & n) != 0
        a = n // 16
        low = sub < 8 - a
        rolled = [[pltpu.roll(t, 8 - a, 0) for t in row] for row in x]
        x = [
            [
                jnp.where(on, jnp.where(low, rolled[c][v], rolled[min(c + 1, 4)][v]), x[c][v])
                for v in range(16)
            ]
            for c in range(5)
        ]
    low = sub < 7
    for n in (8, 4, 2, 1):
        on = (turn & n) != 0
        rolled = [[pltpu.roll(row[v], 7, 0) for v in range(n)] for row in x]
        out = []
        for c in range(5 if n > 1 else 4):
            row = []
            for v in range(16):
                if v + n < 16:
                    moved = x[c][v + n]
                else:
                    moved = jnp.where(low, rolled[c][v + n - 16], rolled[min(c + 1, 4)][v + n - 16])
                row.append(jnp.where(on, moved, x[c][v]))
            out.append(row)
        x = out
    return x


def index_kernel(owner_ref, cell_ref, weight_ref, key_ref, load_ref, start_ref, cells_ref):
    lane = lax.broadcasted_iota(I32, (8, 128), 1)
    sub = lax.broadcasted_iota(I32, (8, 128), 0)
    keys, loads = [], []
    for l in range(4):
        for j in range(4):
            rows = pl.ds(8 * j, 8)
            place = (8 * j + sub) * 128 + lane
            keys.append((owner_ref[l, rows, :] << 23) | (cell_ref[l, rows, :] << 12) | place)
            loads.append(weight_ref[l, rows, :])
    keys, loads = sort_links(keys, loads)
    start = owner_starts(keys)
    start_ref[...] = start
    for v in range(16):
        key_ref[pl.ds(8 * v, 8), :] = keys[v]
        load_ref[pl.ds(8 * v, 8), :] = loads[v]
    cells = [((k >> 12) & 2047).astype(F32) for k in keys]
    slots = owner_slots(cells, start)
    for c in range(4):
        cells_ref[c] = jnp.concatenate(slots[c], axis=0).T


def index_call(owner, cell, weight):
    vm = pl.BlockSpec(memory_space=pltpu.VMEM)
    return pl.pallas_call(
        index_kernel,
        out_shape=(
            jax.ShapeDtypeStruct((128, 128), I32),
            jax.ShapeDtypeStruct((128, 128), F32),
            jax.ShapeDtypeStruct((8, 128), I32),
            jax.ShapeDtypeStruct((4, 128, 128), F32),
        ),
        in_specs=[vm] * 3,
        out_specs=(vm,) * 4,
    )(owner, cell, weight)

BF16 = jnp.bfloat16


def link_values(surf_ref, key_ref, load_ref):
    keys = [key_ref[pl.ds(8 * v, 8), :] for v in range(16)]
    lanes = [k & 127 for k in keys]
    rows = [(k >> 7) & 31 for k in keys]
    found = [[jnp.zeros((8, 128), F32)] * 16 for _ in range(2)]
    for r in range(32):
        table = [jnp.broadcast_to(surf_ref[f, r : r + 1, :], (8, 128)) for f in range(2)]
        for v in range(16):
            here = rows[v] == r
            for f in range(2):
                found[f][v] = jnp.where(here, lanes_of(table[f], lanes[v]), found[f][v])
    loads = [load_ref[pl.ds(8 * v, 8), :] for v in range(16)]
    return [[loads[v] * found[f][v] for v in range(16)] for f in range(2)]


def write_sums(total, out_ref):
    for f in range(2):
        summed = total[32 * f : 32 * f + 16] + total[32 * f + 16 : 32 * f + 32]
        for h in range(16):
            out_ref[f : f + 1, 128 * h : 128 * h + 128] = summed[h : h + 1]


MESH = pl.DeviceIdType.MESH
mixing = 0.1


def at_lane(x, shift):
    return pltpu.roll(x, shift, 1)


def step_kernel(
    n_lat, n_lon,
    temp_hbm, salt_hbm, east_hbm, north_hbm, vdiff_hbm, kmt_ref,
    ft_ref, fs_ref, back_ref,
    tp, sp, vp, up, vd, inv, gain, c_mid, c_east, c_west, c_north, c_south,
    row_up, row_down, col_out, row_up2, row_down2, col_out2,
    g_north, g_south, g_west, g_east, g_north2, g_south2, g_west2, g_east2,
    edge, kp, load_sem, send_sem, recv_sem,
):
    lat, lon = lax.axis_index("lat"), lax.axis_index("lon")
    is_top = lat == n_lat - 1
    has_south = lat > 0
    north_id = (jnp.where(is_top, lat, lat + 1), jnp.where(is_top, n_lon - 1 - lon, lon))
    south_id = (jnp.maximum(lat - 1, 0), lon)
    east_id = (lat, lax.rem(lon + 1, n_lon))
    west_id = (lat, lax.rem(lon + n_lon - 1, n_lon))

    loads = [
        pltpu.make_async_copy(src, dst, load_sem.at[i])
        for i, (src, dst) in enumerate(
            (
                (temp_hbm, tp.at[:, 8:40, :]),
                (salt_hbm, sp.at[:, 8:40, :]),
                (east_hbm, up),
                (north_hbm, vp.at[:, 8:40, :]),
                (vdiff_hbm, vd),
            )
        )
    ]
    for load in loads:
        load.start()

    barrier = pltpu.get_barrier_semaphore()
    for peer in (north_id, east_id, west_id):
        pl.semaphore_signal(barrier, inc=1, device_id=peer, device_id_type=MESH)

    @pl.when(has_south)
    def _():
        pl.semaphore_signal(barrier, inc=1, device_id=south_id, device_id_type=MESH)

    @pl.when(jnp.logical_not(has_south))
    def _():
        g_south[...] = jnp.zeros_like(g_south)
        g_south2[...] = jnp.zeros_like(g_south2)

    lane = lax.broadcasted_iota(I32, (32, 128), 1)
    lane8 = lax.broadcasted_iota(I32, (8, 128), 1)
    kmt = kmt_ref[...].astype(F32)
    kp[8:40, :] = kmt

    def take_rows(src, row, dst, base):
        for g in range(8):
            dst[base + 8 * g : base + 8 * g + 8, :] = src[8 * g : 8 * g + 8, row, :]

    def put_rows(value, dst, g, row):
        dst[8 * g : 8 * g + 8, row, :] = value

    for load in loads[:4]:
        load.wait()
    for base, src in ((0, tp), (64, sp), (136, vp)):
        take_rows(src, 39, row_up, base)
    for base, src in ((0, tp), (64, sp)):
        take_rows(src, 8, row_down, base)
    row_up[128:136, :] = jnp.broadcast_to(kp[39:40, :], (8, 128))
    row_down[128:136, :] = jnp.broadcast_to(kp[8:9, :], (8, 128))

    def pack_level(k, packs):
        pair = (lane >> 1) == k
        fields = (tp[k, 8:40, :], sp[k, 8:40, :], up[k])
        return tuple(
            jnp.where(pair, at_lane(x, 2 * k + 1), p) for x, p in zip(fields, packs)
        )

    zero = jnp.zeros((32, 128), F32)
    packs = lax.fori_loop(0, 64, pack_level, (zero, zero, zero), unroll=4)
    col_out[0:32, :] = packs[0]
    col_out[32:64, :] = packs[1]
    col_out[64:96, :] = at_lane(kmt, 1)
    col_out[96:128, :] = packs[2]

    pl.semaphore_wait(barrier, jnp.where(has_south, 4, 3))

    def exchange(base, up_rows, top_rows, down_rows, east_rows, west_rows, bufs, ghosts):
        row_n, row_s, col = bufs
        north, south, west, east = ghosts

        def copy(src, dst, which, slot, peer):
            return pltpu.make_async_remote_copy(
                src_ref=src, dst_ref=dst, send_sem=send_sem.at[base + which],
                recv_sem=recv_sem.at[base + slot], device_id=peer, device_id_type=MESH,
            )

        to_north = copy(row_n.at[0:up_rows], south.at[0:up_rows], 0, 1, north_id)
        over_fold = copy(row_n.at[0:top_rows], north.at[0:top_rows], 0, 0, north_id)
        to_south = copy(row_s.at[0:down_rows], north.at[0:down_rows], 1, 0, south_id)
        to_east = copy(col.at[0:east_rows], west.at[0:east_rows], 2, 2, east_id)
        to_west = copy(col.at[0:west_rows], east.at[0:west_rows], 3, 3, west_id)

        def start():
            @pl.when(is_top)
            def _():
                over_fold.start()

            @pl.when(jnp.logical_not(is_top))
            def _():
                to_north.start()

            @pl.when(has_south)
            def _():
                to_south.start()

            to_east.start()
            to_west.start()

        def finish():
            @pl.when(is_top)
            def _():
                over_fold.wait_send()

            @pl.when(jnp.logical_not(is_top))
            def _():
                to_north.wait_send()

            @pl.when(has_south)
            def _():
                to_south.wait_send()
                to_north.wait_recv()

            to_south.wait_recv()
            to_east.wait()
            to_west.wait()

        return start, finish

    start, finish = exchange(
        0, 200, 136, 136, 128, 96, (row_up, row_down, col_out), (g_north, g_south, g_west, g_east)
    )
    start()

    loads[4].wait()

    def factor(k, carry):
        above, back = carry
        below = jnp.where((k + 1).astype(F32) < kmt, vd[k], 0.0)
        whole = 1.0 / (1.0 + below + above - above * back)
        inv[k] = whole
        gain[k] = above * whole
        back = below * whole
        back_ref[k] = back
        return below, back

    lax.fori_loop(0, 64, factor, (zero, zero), unroll=4)

    finish()

    mirror = jnp.where(is_top, 127 - lane8, lane8)

    def ghost_rows(north, south, fields):
        for base, dst in fields:
            for g in range(8):
                rows = slice(base + 8 * g, base + 8 * g + 8)
                put_rows(lanes_of(north[rows, :], mirror), dst, g, 40)
                put_rows(south[rows, :], dst, g, 7)

    def ghost_cols(west, east, count):
        for n in range(count):
            rows = slice(32 * n, 32 * n + 32)
            edge[rows, :] = jnp.where(
                (lane & 1) == 0, west[rows, :], at_lane(east[rows, :], 126)
            )

    ghost_rows(g_north, g_south, ((0, tp), (64, sp)))
    for g in range(8):
        put_rows(g_south[136 + 8 * g : 144 + 8 * g, :], vp, g, 7)
    kp[40:48, :] = lanes_of(g_north[128:136, :], mirror)
    kp[0:8, :] = g_south[128:136, :]
    ghost_cols(g_west, g_east, 3)
    edge[96:128, :] = g_west[96:128, :]

    first, last = lane == 0, lane == 127
    kmt_edge = edge[64:96, :]
    wet_east = jnp.minimum(kmt, jnp.where(last, kmt_edge, at_lane(kmt, 127)))
    wet_west = jnp.minimum(kmt, jnp.where(first, kmt_edge, at_lane(kmt, 1)))
    wet_north = jnp.minimum(kmt, kp[9:41, :])
    wet_south = jnp.minimum(kmt, kp[7:39, :])

    def stencil(src, row, k, turn, coefs):
        mid, east, west, north, south = coefs
        here = src[k, 8:40, :]
        ghost = at_lane(edge[row : row + 32, :], turn)
        on_east = jnp.where(last, ghost, at_lane(here, 127))
        on_west = jnp.where(first, ghost, at_lane(here, 1))
        return (
            mid * here + east * on_east + west * on_west
            + north * src[k, 9:41, :] + south * src[k, 7:39, :]
        )

    def down_first(k, carry):
        turn = lax.rem(128 - 2 * k, 128)
        level = k.astype(F32)
        whole = inv[k]
        half_e = 0.5 * up[k]
        half_w = jnp.where(first, 0.5 * at_lane(edge[96:128, :], turn), at_lane(half_e, 1))
        half_n = 0.5 * vp[k, 8:40, :]
        half_s = 0.5 * vp[k, 7:39, :]
        on_e, on_w = level < wet_east, level < wet_west
        on_n, on_s = level < wet_north, level < wet_south
        east = jnp.where(on_e, mixing - half_e, 0.0)
        west = jnp.where(on_w, mixing + half_w, 0.0)
        north = jnp.where(on_n, mixing - half_n, 0.0)
        south = jnp.where(on_s, mixing + half_s, 0.0)
        faces = (
            jnp.where(on_e, 2 * mixing, 0.0) + jnp.where(on_w, 2 * mixing, 0.0)
        ) + (jnp.where(on_n, 2 * mixing, 0.0) + jnp.where(on_s, 2 * mixing, 0.0))
        mid = (1.0 + (((east + west) + (north + south)) - faces)) * whole
        east, west, north, south = east * whole, west * whole, north * whole, south * whole
        c_mid[k], c_east[k], c_west[k], c_north[k], c_south[k] = mid, east, west, north, south
        coefs = (mid, east, west, north, south)
        above = gain[k]
        ft = stencil(tp, 0, k, turn, coefs) + above * carry[0]
        fs = stencil(sp, 32, k, turn, coefs) + above * carry[1]
        ft_ref[k] = ft
        fs_ref[k] = fs
        return ft, fs

    lax.fori_loop(0, 64, down_first, (zero, zero), unroll=2)

    def up_first(i, carry):
        xt, xs, pack_t, pack_s = carry
        k = 63 - i
        back = back_ref[k]
        xt = ft_ref[k] + back * xt
        xs = fs_ref[k] + back * xs
        tp[k, 8:40, :] = xt
        sp[k, 8:40, :] = xs
        pair = (lane >> 1) == k
        pack_t = jnp.where(pair, at_lane(xt, 2 * k + 1), pack_t)
        pack_s = jnp.where(pair, at_lane(xs, 2 * k + 1), pack_s)
        return xt, xs, pack_t, pack_s

    _, _, pack_t, pack_s = lax.fori_loop(0, 64, up_first, (zero, zero, zero, zero), unroll=4)
    col_out2[0:32, :] = pack_t
    col_out2[32:64, :] = pack_s
    for base, src in ((0, tp), (64, sp)):
        take_rows(src, 39, row_up2, base)
        take_rows(src, 8, row_down2, base)

    start, finish = exchange(
        4, 128, 128, 128, 64, 64,
        (row_up2, row_down2, col_out2), (g_north2, g_south2, g_west2, g_east2),
    )
    start()
    finish()
    ghost_rows(g_north2, g_south2, ((0, tp), (64, sp)))
    ghost_cols(g_west2, g_east2, 2)

    def down_second(k, carry):
        turn = lax.rem(128 - 2 * k, 128)
        coefs = (c_mid[k], c_east[k], c_west[k], c_north[k], c_south[k])
        above = gain[k]
        ft = stencil(tp, 0, k, turn, coefs) + above * carry[0]
        fs = stencil(sp, 32, k, turn, coefs) + above * carry[1]
        ft_ref[k] = ft
        fs_ref[k] = fs
        return ft, fs

    lax.fori_loop(0, 64, down_second, (zero, zero), unroll=2)


def step_call(n_lat, n_lon, temp, salt, east, north, vdiff, kmt):
    vm = pl.BlockSpec(memory_space=pltpu.VMEM)
    hbm = pl.BlockSpec(memory_space=pl.ANY)
    field = jax.ShapeDtypeStruct((64, 32, 128), F32)
    block, wide = pltpu.VMEM((64, 32, 128), F32), pltpu.VMEM((64, 48, 128), F32)
    rows = lambda n: pltpu.VMEM((n, 128), F32)
    return pl.pallas_call(
        functools.partial(step_kernel, n_lat, n_lon),
        out_shape=(field,) * 3,
        in_specs=[hbm] * 5 + [vm],
        out_specs=(vm,) * 3,
        scratch_shapes=[wide, wide, wide, block, block, block, block]
        + [block] * 5
        + [rows(n) for n in (200, 136, 128, 128, 128, 64)]
        + [rows(n) for n in (136, 200, 128, 96, 128, 128, 64, 64)]
        + [rows(128), rows(48)]
        + [pltpu.SemaphoreType.DMA((5,)), pltpu.SemaphoreType.DMA((8,)), pltpu.SemaphoreType.DMA((8,))],
        compiler_params=pltpu.CompilerParams(
            collective_id=1, has_side_effects=True, vmem_limit_bytes=48 << 20
        ),
    )(temp, salt, east, north, vdiff, kmt)


def back_kernel(ft_ref, fs_ref, back_ref, kmt_ref, t_ref, s_ref, surf_ref):
    def level(i, carry):
        k = 63 - i
        back = back_ref[k]
        xt = ft_ref[k] + back * carry[0]
        xs = fs_ref[k] + back * carry[1]
        t_ref[k] = xt
        s_ref[k] = xs
        return xt, xs

    zero = jnp.zeros((32, 128), F32)
    xt, xs = lax.fori_loop(0, 64, level, (zero, zero), unroll=4)
    wet = jnp.where(kmt_ref[...] > 0, 1.0, 0.0)
    surf_ref[0] = xt * wet
    surf_ref[1] = xs * wet


def back_call(ft, fs, back, kmt):
    vm = pl.BlockSpec(memory_space=pltpu.VMEM)
    field = jax.ShapeDtypeStruct((64, 32, 128), F32)
    return pl.pallas_call(
        back_kernel,
        out_shape=(field, field, jax.ShapeDtypeStruct((2, 32, 128), F32)),
        in_specs=[vm] * 4,
        out_specs=(vm,) * 3,
        compiler_params=pltpu.CompilerParams(vmem_limit_bytes=48 << 20),
    )(ft, fs, back, kmt)


GROUP = 16


def group_operands(recv_ref, first):
    high_id = lax.broadcasted_iota(I32, (16, 128), 0).astype(F32).astype(BF16)
    low_id = lax.broadcasted_iota(I32, (128, 128), 0).astype(F32).astype(BF16)
    left, right = [], []
    for q in range(GROUP):
        block = recv_ref[first + q]
        cell = block[8:12]
        high = jnp.floor(cell * (1.0 / 128.0))
        low = cell - 128.0 * high
        values = block[0:8]
        coarse = values.astype(BF16).astype(F32)
        fine = values - coarse
        for c in range(4):
            hits = jnp.broadcast_to(high[c : c + 1], (16, 128)).astype(BF16) == high_id
            part = []
            for f in range(2):
                for piece in (coarse, fine):
                    row = jnp.broadcast_to(piece[4 * f + c : 4 * f + c + 1], (16, 128)).astype(BF16)
                    part.append(jnp.where(hits, row, jnp.zeros_like(row)))
            left.append(jnp.concatenate(part, axis=0))
            match = jnp.broadcast_to(low[c : c + 1], (128, 128)).astype(BF16) == low_id
            right.append(jnp.where(match, jnp.ones((128, 128), BF16), jnp.zeros((128, 128), BF16)))
    return jnp.concatenate(left, axis=1), jnp.concatenate(right, axis=1)


def regrid_kernel(
    n_lat, n_lon, surf_ref, key_ref, load_ref, start_ref, cells_ref, out_ref,
    send, recv, ready, send_sem, recv_sem,
):
    n = n_lat * n_lon
    lat, lon = lax.axis_index("lat"), lax.axis_index("lon")
    me = lat * n_lon + lon
    barrier = pltpu.get_barrier_semaphore()

    def signal_lat(d, _):
        peer = (lax.rem(lat + d, n_lat), lon)
        pl.semaphore_signal(barrier, inc=1, device_id=peer, device_id_type=MESH)
        return 0

    def signal_lon(sem):
        def one(d, _):
            peer = (lat, lax.rem(lon + d, n_lon))
            pl.semaphore_signal(sem, inc=1, device_id=peer, device_id_type=MESH)
            return 0

        lax.fori_loop(1, n_lon, one, 0)

    lax.fori_loop(1, n_lat, signal_lat, 0)
    signal_lon(barrier)

    lane = lax.broadcasted_iota(I32, (8, 128), 1)
    sub = lax.broadcasted_iota(I32, (8, 128), 0)
    start = start_ref[...]
    after = jnp.where(lane < 127, pltpu.roll(start, 127, 1), 16384)
    count = after - start
    values = link_values(surf_ref, key_ref, load_ref)
    for c in range(4):
        send[:, 8 + c, :] = cells_ref[c]

    pl.semaphore_wait(barrier, n_lat + n_lon - 2)
    signal_lon(ready)

    for f in range(2):
        slots = owner_slots(values[f], start)
        for c in range(4):
            kept = [
                jnp.where(sub * 16 + (c * 128 + v) < count, slots[c][v], 0.0) for v in range(16)
            ]
            send[:, 4 * f + c, :] = jnp.concatenate(kept, axis=0).T

    pl.semaphore_wait(ready, n_lon - 1)

    def send_one(d, _):
        to = lax.rem(me + d, n)
        pltpu.make_async_remote_copy(
            src_ref=send.at[to], dst_ref=recv.at[d], send_sem=send_sem,
            recv_sem=recv_sem.at[d // GROUP],
            device_id=(to // n_lon, lax.rem(to, n_lon)), device_id_type=MESH,
        ).start()
        return 0

    lax.fori_loop(1, n, send_one, 0)
    recv[0] = send[me]

    def arrived(lo, hi, g):
        part = recv.at[lo:hi] if isinstance(lo, int) else recv.at[pl.ds(lo, hi)]
        pltpu.make_async_copy(part, part, recv_sem.at[g]).wait()

    def add_group(g, total):
        @pl.when(g == 0)
        def _():
            arrived(1, GROUP, 0)

        @pl.when(g > 0)
        def _():
            arrived(pl.multiple_of(g * GROUP, GROUP), GROUP, g)

        left, right = group_operands(recv, g * GROUP)
        return total + lax.dot_general(
            right, left, (((1,), (1,)), ((), ())), preferred_element_type=F32
        )

    total = lax.fori_loop(0, n // GROUP, add_group, jnp.zeros((128, 64), F32))
    write_sums(total.T, out_ref)
    sent = send.at[0 : n - 1]
    pltpu.make_async_copy(sent, sent, send_sem).wait()


def regrid_call(n_lat, n_lon, surf, key, load, start, cells):
    vm = pl.BlockSpec(memory_space=pltpu.VMEM)
    n = n_lat * n_lon
    return pl.pallas_call(
        functools.partial(regrid_kernel, n_lat, n_lon),
        out_shape=jax.ShapeDtypeStruct((2, 2048), F32),
        in_specs=[vm] * 5,
        out_specs=vm,
        scratch_shapes=[
            pltpu.VMEM((128, 12, 128), F32),
            pltpu.VMEM((128, 12, 128), F32),
            pltpu.SemaphoreType.REGULAR,
            pltpu.SemaphoreType.DMA,
            pltpu.SemaphoreType.DMA((n // GROUP,)),
        ],
        compiler_params=pltpu.CompilerParams(
            collective_id=2, has_side_effects=True, vmem_limit_bytes=32 << 20
        ),
    )(surf, key, load, start, cells)


def solution(mesh):
    n_lat, n_lon = mesh.shape["lat"], mesh.shape["lon"]

    def body(temp, salt, u_east, v_north, vdiff, kmt, owner, atmo_cell, weight):
        key, load, start, cells = index_call(owner, atmo_cell, weight)
        ft, fs, back = step_call(n_lat, n_lon, temp, salt, u_east, v_north, vdiff, kmt)
        t_out, s_out, surf = back_call(ft, fs, back, kmt)
        atmo = regrid_call(n_lat, n_lon, surf, key, load, start, cells)
        return t_out, s_out, atmo

    level, flat = P(None, "lat", "lon"), P("lat", "lon")
    return jax.shard_map(
        body,
        mesh=mesh,
        in_specs=(level,) * 5 + (flat,) + (level,) * 3,
        out_specs=(level, level, P(None, ("lat", "lon"))),
        check_vma=False,
    )
```

profile of v0, /device:TPU:1, one launch (start us, length us, event | category | flops | bytes accessed | tf_op | source)
XLA Modules:
  0.0 67.7 jit_solution(12541447815116993008)
XLA Ops:
  0.6 0.0 copy-start
  0.6 1.2 %copy-done = f32[64,32,128]{2,1,0:T(8,128)S(1)} copy-done((f32[64,32,128]{2,1,0:T(8,128)S(1)}, f32[64,32,128]{2,1,0:T(8,128)}, u32[]{:S(2)}) %copy-start) | copy-done | bytes 1048600
  1.9 0.0 copy-start.1
  1.9 1.2 %copy-done.1 = f32[64,32,128]{2,1,0:T(8,128)S(1)} copy-done((f32[64,32,128]{2,1,0:T(8,128)S(1)}, f32[64,32,128]{2,1,0:T(8,128)}, u32[]{:S(2)}) %copy-start.1) | copy-done | bytes 1048600
  3.1 0.0 copy-start.3
  3.1 0.7 %copy-done.3 = s32[32,128]{1,0:T(8,128)S(1)} copy-done((s32[32,128]{1,0:T(8,128)S(1)}, s32[32,128]{1,0:T(8,128)}, u32[]{:S(2)}) %copy-start.3) | copy-done | bytes 16408
  3.8 27.8 %shard_map.112 = (f32[64,32,128]{2,1,0:T(8,128)S(1)}, f32[64,32,128]{2,1,0:T(8,128)S(1)}, f32[64,32,128]{2,1,0:T(8,128)S(1)}) custom-call(f32[64,32,128]{2,1,0:T(8,128)S(1)} %copy-done, f32[64,32,128]{2,1,0:T(8,128)S(1)} %copy-done.1, f32[64,32,128]{2,1,0:T(8,128)} %east_hbm.1, f32[64,32,128]{2,1,0:T(8,128)} %north_hbm.1, f32[64,32,128]{2,1,0:T(8,128)} %vdiff_hbm.1, ...), custom_call_target="tpu_custom_call" | custom-call | tf_op jit(solution)/shard_map/pallas_call | solution.py:480
  31.6 1.6 %shard_map.113 = (f32[64,32,128]{2,1,0:T(8,128)}, f32[64,32,128]{2,1,0:T(8,128)}, f32[2,32,128]{2,1,0:T(8,128)S(1)}) custom-call(f32[64,32,128]{2,1,0:T(8,128)S(1)} %get-tuple-element.13.ft_ref, f32[64,32,128]{2,1,0:T(8,128)S(1)} %get-tuple-element.14.fs_ref, f32[64,32,128]{2,1,0:T(8,128)S(1)} %get-tuple-element.15.back_ref, s32[32,128]{1,0:T(8,128)S(1)} %copy-done.3), custom_call_target="tpu_custom_call" | custom-call | tf_op jit(solution)/shard_map/pallas_call | solution.py:517
  33.2 6.2 %shard_map.114 = (s32[128,128]{1,0:T(8,128)}, f32[128,128]{1,0:T(8,128)}, s32[8,128]{1,0:T(8,128)}, f32[4,128,128]{2,1,0:T(8,128)}) custom-call(s32[4,32,128]{2,1,0:T(8,128)} %owner_ref.1, s32[4,32,128]{2,1,0:T(8,128)} %cell_ref.1, f32[4,32,128]{2,1,0:T(8,128)} %weight_ref.1), custom_call_target="tpu_custom_call" | custom-call | tf_op jit(solution)/shard_map/pallas_call | solution.py:160
  39.4 0.0 copy-start.6
  39.4 0.7 %copy-done.6 = s32[8,128]{1,0:T(8,128)S(1)} copy-done((s32[8,128]{1,0:T(8,128)S(1)}, s32[8,128]{1,0:T(8,128)}, u32[]{:S(2)}) %copy-start.6) | copy-done | bytes 4120
  40.1 0.0 copy-start.2
  40.1 0.9 %copy-done.2 = f32[4,128,128]{2,1,0:T(8,128)S(1)} copy-done((f32[4,128,128]{2,1,0:T(8,128)S(1)}, f32[4,128,128]{2,1,0:T(8,128)}, u32[]{:S(2)}) %copy-start.2) | copy-done | bytes 262168
  41.0 0.0 copy-start.4
  41.0 0.8 %copy-done.4 = s32[128,128]{1,0:T(8,128)S(1)} copy-done((s32[128,128]{1,0:T(8,128)S(1)}, s32[128,128]{1,0:T(8,128)}, u32[]{:S(2)}) %copy-start.4) | copy-done | bytes 65560
  41.9 0.0 copy-start.5
  41.9 0.8 %copy-done.5 = f32[128,128]{1,0:T(8,128)S(1)} copy-done((f32[128,128]{1,0:T(8,128)S(1)}, f32[128,128]{1,0:T(8,128)}, u32[]{:S(2)}) %copy-start.5) | copy-done | bytes 65560
  42.7 24.4 %shard_map.115 = f32[2,2048]{1,0:T(2,128)S(1)} custom-call(f32[2,32,128]{2,1,0:T(8,128)S(1)} %get-tuple-element.18.surf_ref, s32[128,128]{1,0:T(8,128)S(1)} %copy-done.4, f32[128,128]{1,0:T(8,128)S(1)} %copy-done.5, s32[8,128]{1,0:T(8,128)S(1)} %copy-done.6, f32[4,128,128]{2,1,0:T(8,128)S(1)} %copy-done.2), custom_call_target="tpu_custom_call" | custom-call | tf_op jit(solution)/shard_map/pallas_call | solution.py:640
  67.1 0.6 copy.13
Async XLA Ops:
  0.6 1.2 %copy-start = (f32[64,32,128]{2,1,0:T(8,128)S(1)}, f32[64,32,128]{2,1,0:T(8,128)}, u32[]{:S(2)}) copy-start(f32[64,32,128]{2,1,0:T(8,128)} %temp_hbm.1) | copy-start | bytes 3145732
  1.9 1.2 %copy-start.1 = (f32[64,32,128]{2,1,0:T(8,128)S(1)}, f32[64,32,128]{2,1,0:T(8,128)}, u32[]{:S(2)}) copy-start(f32[64,32,128]{2,1,0:T(8,128)} %salt_hbm.1) | copy-start | bytes 3145732
  3.1 0.7 %copy-start.3 = (s32[32,128]{1,0:T(8,128)S(1)}, s32[32,128]{1,0:T(8,128)}, u32[]{:S(2)}) copy-start(s32[32,128]{1,0:T(8,128)} %kmt_ref.3) | copy-start | bytes 49156
  39.4 0.7 %copy-start.6 = (s32[8,128]{1,0:T(8,128)S(1)}, s32[8,128]{1,0:T(8,128)}, u32[]{:S(2)}) copy-start(s32[8,128]{1,0:T(8,128)} %get-tuple-element.21.start_ref) | copy-start | bytes 12292
  40.1 0.9 %copy-start.2 = (f32[4,128,128]{2,1,0:T(8,128)S(1)}, f32[4,128,128]{2,1,0:T(8,128)}, u32[]{:S(2)}) copy-start(f32[4,128,128]{2,1,0:T(8,128)} %get-tuple-element.22.cells_ref) | copy-start | bytes 786436
  41.0 0.8 %copy-start.4 = (s32[128,128]{1,0:T(8,128)S(1)}, s32[128,128]{1,0:T(8,128)}, u32[]{:S(2)}) copy-start(s32[128,128]{1,0:T(8,128)} %get-tuple-element.19.key_ref) | copy-start | bytes 196612
  41.9 0.8 %copy-start.5 = (f32[128,128]{1,0:T(8,128)S(1)}, f32[128,128]{1,0:T(8,128)}, u32[]{:S(2)}) copy-start(f32[128,128]{1,0:T(8,128)} %get-tuple-element.20.load_ref) | copy-start | bytes 196612
where the time goes:
time: 68.2 us; the launch traced here: 67.7 us
  Pallas kernels  60 us (88%)
  local copies, waits for them, and re-layouts  7.08 us (10%)
    pallas_call x1, Pallas kernels, step_call(): pl.pallas_call(functools.partial(step_kernel, n_lat, n_lon), out_shape=(f...  27.8 us
    pallas_call x1, Pallas kernels, regrid_call(): pl.pallas_call(functools.partial(regrid_kernel, n_lat, n_lon), out_shape=...  24.4 us
    unnamed x15, local copies, waits for them, and re-layouts  7.08 us
    pallas_call x1, Pallas kernels, index_call(): pl.pallas_call(index_kernel, out_shape=(jax.ShapeDtypeStruct((128, 128),...  6.16 us
    pallas_call x1, Pallas kernels, back_call(): pl.pallas_call(back_kernel, out_shape=(field, field, jax.ShapeDtypeStruct...  1.61 us

commit v1 on v0

v1 whole, which is shorter than its diff:
```python
import functools

import jax
import jax.numpy as jnp
from jax import lax
from jax.experimental import pallas as pl
from jax.experimental.pallas import tpu as pltpu
from jax.sharding import PartitionSpec as P

I32 = jnp.int32
F32 = jnp.float32
BF16 = jnp.bfloat16
MESH = pl.DeviceIdType.MESH
mixing = 0.1
GROUP = 16
FIRST_MERGES = 12
VMEM_MB = 60
HAND_MB = 60


def lanes_of(x, idx):
    return jnp.take_along_axis(x, idx, axis=1, mode="promise_in_bounds")


def owner_starts(keys):
    lane = lax.broadcasted_iota(I32, (8, 128), 1)
    first = jnp.broadcast_to(keys[0][0:1, :], (8, 128))
    bound = lane << 23
    count = jnp.zeros((8, 128), I32)
    for step in (128, 64, 32, 16, 8, 4, 2, 1):
        trial = count + step
        value = lanes_of(first, jnp.minimum(trial - 1, 127))
        fits = jnp.logical_and(trial <= 128, value < bound)
        count = jnp.where(fits, trial, count)
    column = jnp.maximum(count - 1, 0)
    within = jnp.zeros((8, 128), I32)
    for v in range(16):
        within = within + jnp.where(lanes_of(keys[v], column) < bound, 1, 0)
    within = jnp.broadcast_to(jnp.sum(within, axis=0, keepdims=True), (8, 128))
    return jnp.where(count > 0, column * 128 + within, 0)


def owner_slots(tiles, start):
    sub = lax.broadcasted_iota(I32, (8, 128), 0)
    column = start >> 7
    turn = start & 127
    x = []
    for c in range(5):
        idx = jnp.minimum(column + c, 127)
        x.append([lanes_of(tiles[v], idx) for v in range(16)])
    for n in (64, 32, 16):
        on = (turn & n) != 0
        a = n // 16
        low = sub < 8 - a
        rolled = [[pltpu.roll(t, 8 - a, 0) for t in row] for row in x]
        x = [
            [
                jnp.where(on, jnp.where(low, rolled[c][v], rolled[min(c + 1, 4)][v]), x[c][v])
                for v in range(16)
            ]
            for c in range(5)
        ]
    low = sub < 7
    for n in (8, 4, 2, 1):
        on = (turn & n) != 0
        rolled = [[pltpu.roll(row[v], 7, 0) for v in range(n)] for row in x]
        out = []
        for c in range(5 if n > 1 else 4):
            row = []
            for v in range(16):
                if v + n < 16:
                    moved = x[c][v + n]
                else:
                    moved = jnp.where(low, rolled[c][v + n - 16], rolled[min(c + 1, 4)][v + n - 16])
                row.append(jnp.where(on, moved, x[c][v]))
            out.append(row)
        x = out
    return x


def link_values(surf_ref, key_ref, load_ref):
    keys = [key_ref[pl.ds(8 * v, 8), :] for v in range(16)]
    lanes = [k & 127 for k in keys]
    rows = [(k >> 7) & 31 for k in keys]
    found = [[jnp.zeros((8, 128), F32)] * 16 for _ in range(2)]
    for r in range(32):
        table = [jnp.broadcast_to(surf_ref[f, r : r + 1, :], (8, 128)) for f in range(2)]
        for v in range(16):
            here = rows[v] == r
            for f in range(2):
                found[f][v] = jnp.where(here, lanes_of(table[f], lanes[v]), found[f][v])
    loads = [load_ref[pl.ds(8 * v, 8), :] for v in range(16)]
    return [[loads[v] * found[f][v] for v in range(16)] for f in range(2)]


def write_sums(total, out_ref):
    for f in range(2):
        summed = total[32 * f : 32 * f + 16] + total[32 * f + 16 : 32 * f + 32]
        for h in range(16):
            out_ref[f : f + 1, 128 * h : 128 * h + 128] = summed[h : h + 1]


def at_lane(x, shift):
    return pltpu.roll(x, shift, 1)


def group_operands(recv_ref, first):
    high_id = lax.broadcasted_iota(I32, (16, 128), 0).astype(F32).astype(BF16)
    low_id = lax.broadcasted_iota(I32, (128, 128), 0).astype(F32).astype(BF16)
    left, right = [], []
    for q in range(GROUP):
        block = recv_ref[first + q]
        cell = block[8:12]
        high = jnp.floor(cell * (1.0 / 128.0))
        low = cell - 128.0 * high
        values = block[0:8]
        coarse = values.astype(BF16).astype(F32)
        fine = values - coarse
        for c in range(4):
            hits = jnp.broadcast_to(high[c : c + 1], (16, 128)).astype(BF16) == high_id
            part = []
            for f in range(2):
                for piece in (coarse, fine):
                    row = jnp.broadcast_to(piece[4 * f + c : 4 * f + c + 1], (16, 128)).astype(BF16)
                    part.append(jnp.where(hits, row, jnp.zeros_like(row)))
            left.append(jnp.concatenate(part, axis=0))
            match = jnp.broadcast_to(low[c : c + 1], (128, 128)).astype(BF16) == low_id
            right.append(jnp.where(match, jnp.ones((128, 128), BF16), jnp.zeros((128, 128), BF16)))
    return jnp.concatenate(left, axis=1), jnp.concatenate(right, axis=1)


def merges(keys, loads, tops):
    lane = lax.broadcasted_iota(I32, (8, 128), 1)
    sub = lax.broadcasted_iota(I32, (8, 128), 0)

    def bit(b):
        if b < 4 or b >= 14:
            return None
        where = sub >> (b - 4) if b < 7 else lane >> (b - 7)
        return (where & 1) == 1

    for top in tops:
        for b in range(top - 1, -1, -1):
            down = bit(top)
            new_k, new_w = list(keys), list(loads)
            if b < 4:
                for v in range(16):
                    if (v >> b) & 1:
                        continue
                    u = v | (1 << b)
                    if top < 4 and (v >> top) & 1:
                        swap = keys[v] < keys[u]
                    else:
                        swap = keys[v] > keys[u]
                    if down is not None:
                        swap = jnp.logical_xor(swap, down)
                    new_k[v] = jnp.where(swap, keys[u], keys[v])
                    new_k[u] = jnp.where(swap, keys[v], keys[u])
                    new_w[v] = jnp.where(swap, loads[u], loads[v])
                    new_w[u] = jnp.where(swap, loads[v], loads[u])
            else:
                keep_max = bit(b) if down is None else jnp.logical_xor(bit(b), down)
                if b < 7:
                    idx, axis = sub ^ (1 << (b - 4)), 0
                else:
                    idx, axis = lane ^ (1 << (b - 7)), 1
                for v in range(16):
                    k, w = keys[v], loads[v]
                    pk = jnp.take_along_axis(k, idx, axis=axis, mode="promise_in_bounds")
                    pw = jnp.take_along_axis(w, idx, axis=axis, mode="promise_in_bounds")
                    take = jnp.logical_or(
                        jnp.logical_and(keep_max, pk > k),
                        jnp.logical_and(jnp.logical_not(keep_max), pk < k),
                    )
                    new_k[v] = jnp.where(take, pk, k)
                    new_w[v] = jnp.where(take, pw, w)
            keys, loads = new_k, new_w
    return keys, loads


def whole_kernel(
    n_lat, n_lon,
    temp_hbm, salt_hbm, east_hbm, north_hbm, vdiff_hbm, kmt_ref, owner_hbm, cell_hbm, weight_hbm,
    t_hbm, s_hbm, atmo_ref,
    t_ref, s_ref, tp, sp, vp, up, vd, inv, gain, back_ref, c_mid, c_east, c_west, c_north, c_south,
    row_up, row_down, col_out, row_up2, row_down2, col_out2,
    g_north, g_south, g_west, g_east, g_north2, g_south2, g_west2, g_east2,
    edge, kp, owner_ref, cell_ref, weight_ref, key_ref, load_ref, surf_ref, send, recv,
    load_sem, store_sem, send_sem, recv_sem, ready, all_send, all_recv,
):
    n = n_lat * n_lon
    lat, lon = lax.axis_index("lat"), lax.axis_index("lon")
    me = lat * n_lon + lon
    is_top = lat == n_lat - 1
    has_south = lat > 0
    north_id = (jnp.where(is_top, lat, lat + 1), jnp.where(is_top, n_lon - 1 - lon, lon))
    south_id = (jnp.maximum(lat - 1, 0), lon)
    east_id = (lat, lax.rem(lon + 1, n_lon))
    west_id = (lat, lax.rem(lon + n_lon - 1, n_lon))

    loads = [
        pltpu.make_async_copy(src, dst, load_sem.at[i])
        for i, (src, dst) in enumerate(
            (
                (temp_hbm, tp.at[:, 8:40, :]),
                (salt_hbm, sp.at[:, 8:40, :]),
                (east_hbm, up),
                (north_hbm, vp.at[:, 8:40, :]),
                (vdiff_hbm, vd),
                (owner_hbm, owner_ref),
                (cell_hbm, cell_ref),
                (weight_hbm, weight_ref),
            )
        )
    ]
    for load in loads:
        load.start()

    barrier = pltpu.get_barrier_semaphore()

    def greet_row(sem):
        def one(d, _):
            peer = (lat, lax.rem(lon + d, n_lon))
            pl.semaphore_signal(sem, inc=1, device_id=peer, device_id_type=MESH)
            return 0

        lax.fori_loop(1, n_lon, one, 0)

    def greet_column(d, _):
        peer = (lax.rem(lat + d, n_lat), lon)
        pl.semaphore_signal(barrier, inc=1, device_id=peer, device_id_type=MESH)
        return 0

    lax.fori_loop(1, n_lat, greet_column, 0)
    greet_row(barrier)

    @pl.when(jnp.logical_not(has_south))
    def _():
        g_south[...] = jnp.zeros_like(g_south)
        g_south2[...] = jnp.zeros_like(g_south2)

    lane = lax.broadcasted_iota(I32, (32, 128), 1)
    lane8 = lax.broadcasted_iota(I32, (8, 128), 1)
    sub8 = lax.broadcasted_iota(I32, (8, 128), 0)
    kmt = kmt_ref[...].astype(F32)
    kp[8:40, :] = kmt

    def take_rows(src, row, dst, base):
        for g in range(8):
            dst[base + 8 * g : base + 8 * g + 8, :] = src[8 * g : 8 * g + 8, row, :]

    def put_rows(value, dst, g, row):
        dst[8 * g : 8 * g + 8, row, :] = value

    for load in loads[:4]:
        load.wait()
    for base, src in ((0, tp), (64, sp), (136, vp)):
        take_rows(src, 39, row_up, base)
    for base, src in ((0, tp), (64, sp)):
        take_rows(src, 8, row_down, base)
    row_up[128:136, :] = jnp.broadcast_to(kp[39:40, :], (8, 128))
    row_down[128:136, :] = jnp.broadcast_to(kp[8:9, :], (8, 128))

    def pack_level(k, packs):
        pair = (lane >> 1) == k
        fields = (tp[k, 8:40, :], sp[k, 8:40, :], up[k])
        return tuple(
            jnp.where(pair, at_lane(x, 2 * k + 1), p) for x, p in zip(fields, packs)
        )

    zero = jnp.zeros((32, 128), F32)
    packs = lax.fori_loop(0, 64, pack_level, (zero, zero, zero), unroll=4)
    col_out[0:32, :] = packs[0]
    col_out[32:64, :] = packs[1]
    col_out[64:96, :] = at_lane(kmt, 1)
    col_out[96:128, :] = packs[2]

    pl.semaphore_wait(barrier, n_lat + n_lon - 2)

    def exchange(base, up_rows, top_rows, down_rows, east_rows, west_rows, bufs, ghosts):
        row_n, row_s, col = bufs
        north, south, west, east = ghosts

        def copy(src, dst, which, slot, peer):
            return pltpu.make_async_remote_copy(
                src_ref=src, dst_ref=dst, send_sem=send_sem.at[base + which],
                recv_sem=recv_sem.at[base + slot], device_id=peer, device_id_type=MESH,
            )

        to_north = copy(row_n.at[0:up_rows], south.at[0:up_rows], 0, 1, north_id)
        over_fold = copy(row_n.at[0:top_rows], north.at[0:top_rows], 0, 0, north_id)
        to_south = copy(row_s.at[0:down_rows], north.at[0:down_rows], 1, 0, south_id)
        to_east = copy(col.at[0:east_rows], west.at[0:east_rows], 2, 2, east_id)
        to_west = copy(col.at[0:west_rows], east.at[0:west_rows], 3, 3, west_id)

        def start():
            @pl.when(is_top)
            def _():
                over_fold.start()

            @pl.when(jnp.logical_not(is_top))
            def _():
                to_north.start()

            @pl.when(has_south)
            def _():
                to_south.start()

            to_east.start()
            to_west.start()

        def finish():
            @pl.when(is_top)
            def _():
                over_fold.wait_send()

            @pl.when(jnp.logical_not(is_top))
            def _():
                to_north.wait_send()

            @pl.when(has_south)
            def _():
                to_south.wait_send()
                to_north.wait_recv()

            to_south.wait_recv()
            to_east.wait()
            to_west.wait()

        return start, finish

    start, finish = exchange(
        0, 200, 136, 136, 128, 96, (row_up, row_down, col_out), (g_north, g_south, g_west, g_east)
    )
    start()
    greet_row(ready)

    loads[4].wait()

    def factor(k, carry):
        above, back = carry
        below = jnp.where((k + 1).astype(F32) < kmt, vd[k], 0.0)
        whole = 1.0 / (1.0 + below + above - above * back)
        inv[k] = whole
        gain[k] = above * whole
        back = below * whole
        back_ref[k] = back
        return below, back

    lax.fori_loop(0, 64, factor, (zero, zero), unroll=4)

    for load in loads[5:]:
        load.wait()

    def hold(keys, loads):
        for v in range(16):
            key_ref[8 * v : 8 * v + 8, :] = keys[v]
            load_ref[8 * v : 8 * v + 8, :] = loads[v]

    def held(ref):
        return [ref[8 * v : 8 * v + 8, :] for v in range(16)]

    keys, shares = [], []
    for l in range(4):
        for j in range(4):
            rows = slice(8 * j, 8 * j + 8)
            place = (8 * j + sub8) * 128 + lane8
            keys.append((owner_ref[l, rows, :] << 23) | (cell_ref[l, rows, :] << 12) | place)
            shares.append(weight_ref[l, rows, :])
    hold(*merges(keys, shares, range(1, FIRST_MERGES + 1)))

    finish()

    mirror = jnp.where(is_top, 127 - lane8, lane8)

    def ghost_rows(north, south, fields):
        for base, dst in fields:
            for g in range(8):
                rows = slice(base + 8 * g, base + 8 * g + 8)
                put_rows(lanes_of(north[rows, :], mirror), dst, g, 40)
                put_rows(south[rows, :], dst, g, 7)

    def ghost_cols(west, east, count):
        for i in range(count):
            rows = slice(32 * i, 32 * i + 32)
            edge[rows, :] = jnp.where(
                (lane & 1) == 0, west[rows, :], at_lane(east[rows, :], 126)
            )

    ghost_rows(g_north, g_south, ((0, tp), (64, sp)))
    for g in range(8):
        put_rows(g_south[136 + 8 * g : 144 + 8 * g, :], vp, g, 7)
    kp[40:48, :] = lanes_of(g_north[128:136, :], mirror)
    kp[0:8, :] = g_south[128:136, :]
    ghost_cols(g_west, g_east, 3)
    edge[96:128, :] = g_west[96:128, :]

    first, last = lane == 0, lane == 127
    kmt_edge = edge[64:96, :]
    wet_east = jnp.minimum(kmt, jnp.where(last, kmt_edge, at_lane(kmt, 127)))
    wet_west = jnp.minimum(kmt, jnp.where(first, kmt_edge, at_lane(kmt, 1)))
    wet_north = jnp.minimum(kmt, kp[9:41, :])
    wet_south = jnp.minimum(kmt, kp[7:39, :])

    def stencil(src, row, k, turn, coefs):
        mid, east, west, north, south = coefs
        here = src[k, 8:40, :]
        ghost = at_lane(edge[row : row + 32, :], turn)
        on_east = jnp.where(last, ghost, at_lane(here, 127))
        on_west = jnp.where(first, ghost, at_lane(here, 1))
        return (
            mid * here + east * on_east + west * on_west
            + north * src[k, 9:41, :] + south * src[k, 7:39, :]
        )

    def advance(k, carry, turn, coefs):
        above = gain[k]
        ft = stencil(tp, 0, k, turn, coefs) + above * carry[0]
        fs = stencil(sp, 32, k, turn, coefs) + above * carry[1]
        t_ref[k] = ft
        s_ref[k] = fs
        return ft, fs

    def down_first(k, carry):
        turn = lax.rem(128 - 2 * k, 128)
        level = k.astype(F32)
        whole = inv[k]
        half_e = 0.5 * up[k]
        half_w = jnp.where(first, 0.5 * at_lane(edge[96:128, :], turn), at_lane(half_e, 1))
        half_n = 0.5 * vp[k, 8:40, :]
        half_s = 0.5 * vp[k, 7:39, :]
        on_e, on_w = level < wet_east, level < wet_west
        on_n, on_s = level < wet_north, level < wet_south
        east = jnp.where(on_e, mixing - half_e, 0.0)
        west = jnp.where(on_w, mixing + half_w, 0.0)
        north = jnp.where(on_n, mixing - half_n, 0.0)
        south = jnp.where(on_s, mixing + half_s, 0.0)
        faces = (
            jnp.where(on_e, 2 * mixing, 0.0) + jnp.where(on_w, 2 * mixing, 0.0)
        ) + (jnp.where(on_n, 2 * mixing, 0.0) + jnp.where(on_s, 2 * mixing, 0.0))
        mid = (1.0 + (((east + west) + (north + south)) - faces)) * whole
        east, west, north, south = east * whole, west * whole, north * whole, south * whole
        c_mid[k], c_east[k], c_west[k], c_north[k], c_south[k] = mid, east, west, north, south
        return advance(k, carry, turn, (mid, east, west, north, south))

    lax.fori_loop(0, 64, down_first, (zero, zero), unroll=2)

    def up_first(i, carry):
        xt, xs, pack_t, pack_s = carry
        k = 63 - i
        back = back_ref[k]
        xt = t_ref[k] + back * xt
        xs = s_ref[k] + back * xs
        tp[k, 8:40, :] = xt
        sp[k, 8:40, :] = xs
        pair = (lane >> 1) == k
        pack_t = jnp.where(pair, at_lane(xt, 2 * k + 1), pack_t)
        pack_s = jnp.where(pair, at_lane(xs, 2 * k + 1), pack_s)
        return xt, xs, pack_t, pack_s

    _, _, pack_t, pack_s = lax.fori_loop(0, 64, up_first, (zero, zero, zero, zero), unroll=4)
    col_out2[0:32, :] = pack_t
    col_out2[32:64, :] = pack_s
    for base, src in ((0, tp), (64, sp)):
        take_rows(src, 39, row_up2, base)
        take_rows(src, 8, row_down2, base)

    start, finish = exchange(
        4, 128, 128, 128, 64, 64,
        (row_up2, row_down2, col_out2), (g_north2, g_south2, g_west2, g_east2),
    )
    start()

    keys, shares = merges(held(key_ref), held(load_ref), range(FIRST_MERGES + 1, 15))
    hold(keys, shares)
    begin = owner_starts(keys)
    cells = owner_slots([((k >> 12) & 2047).astype(F32) for k in keys], begin)
    for c in range(4):
        send[:, 8 + c, :] = jnp.concatenate(cells[c], axis=0).T

    finish()
    ghost_rows(g_north2, g_south2, ((0, tp), (64, sp)))
    ghost_cols(g_west2, g_east2, 2)

    def down_second(k, carry):
        turn = lax.rem(128 - 2 * k, 128)
        return advance(k, carry, turn, (c_mid[k], c_east[k], c_west[k], c_north[k], c_south[k]))

    lax.fori_loop(0, 64, down_second, (zero, zero), unroll=2)

    def up_second(i, carry):
        k = 63 - i
        back = back_ref[k]
        xt = t_ref[k] + back * carry[0]
        xs = s_ref[k] + back * carry[1]
        t_ref[k] = xt
        s_ref[k] = xs
        return xt, xs

    xt, xs = lax.fori_loop(0, 64, up_second, (zero, zero), unroll=4)
    stores = [
        pltpu.make_async_copy(t_ref, t_hbm, store_sem.at[0]),
        pltpu.make_async_copy(s_ref, s_hbm, store_sem.at[1]),
    ]
    for store in stores:
        store.start()
    wet = jnp.where(kmt > 0.0, 1.0, 0.0)
    surf_ref[0] = xt * wet
    surf_ref[1] = xs * wet

    values = link_values(surf_ref, key_ref, load_ref)
    count = jnp.where(lane8 < 127, pltpu.roll(begin, 127, 1), 16384) - begin
    for f in range(2):
        slots = owner_slots(values[f], begin)
        for c in range(4):
            kept = [
                jnp.where(sub8 * 16 + (c * 128 + v) < count, slots[c][v], 0.0) for v in range(16)
            ]
            send[:, 4 * f + c, :] = jnp.concatenate(kept, axis=0).T

    pl.semaphore_wait(ready, n_lon - 1)

    def send_one(d, _):
        to = lax.rem(me + d, n)
        pltpu.make_async_remote_copy(
            src_ref=send.at[to], dst_ref=recv.at[d], send_sem=all_send,
            recv_sem=all_recv.at[d // GROUP],
            device_id=(to // n_lon, lax.rem(to, n_lon)), device_id_type=MESH,
        ).start()
        return 0

    lax.fori_loop(1, n, send_one, 0)
    recv[0] = send[me]

    def add_group(g, total):
        @pl.when(g == 0)
        def _():
            part = recv.at[1:GROUP]
            pltpu.make_async_copy(part, part, all_recv.at[0]).wait()

        @pl.when(g > 0)
        def _():
            part = recv.at[pl.ds(pl.multiple_of(g * GROUP, GROUP), GROUP)]
            pltpu.make_async_copy(part, part, all_recv.at[g]).wait()

        left, right = group_operands(recv, g * GROUP)
        return total + lax.dot_general(
            right, left, (((1,), (1,)), ((), ())), preferred_element_type=F32
        )

    total = lax.fori_loop(0, n // GROUP, add_group, jnp.zeros((128, 64), F32))
    write_sums(total.T, atmo_ref)
    for store in stores:
        store.wait()
    sent = send.at[0 : n - 1]
    pltpu.make_async_copy(sent, sent, all_send).wait()


def whole_call(n_lat, n_lon, temp, salt, east, north, vdiff, kmt, owner, cell, weight):
    vm = pl.BlockSpec(memory_space=pltpu.VMEM)
    hbm = pl.BlockSpec(memory_space=pltpu.HBM)
    field = jax.ShapeDtypeStruct((64, 32, 128), F32)
    block, wide = pltpu.VMEM((64, 32, 128), F32), pltpu.VMEM((64, 48, 128), F32)
    links = pltpu.VMEM((4, 32, 128), I32)
    dma = pltpu.SemaphoreType.DMA
    n = n_lat * n_lon

    def rows(count, dtype=F32):
        return pltpu.VMEM((count, 128), dtype)

    return pl.pallas_call(
        functools.partial(whole_kernel, n_lat, n_lon),
        out_shape=(field, field, jax.ShapeDtypeStruct((2, 2048), F32)),
        in_specs=[hbm] * 5 + [vm] + [hbm] * 3,
        out_specs=(hbm, hbm, vm),
        scratch_shapes=[block] * 2
        + [wide] * 3
        + [block] * 10
        + [rows(r) for r in (200, 136, 128, 128, 128, 64)]
        + [rows(r) for r in (136, 200, 128, 96, 128, 128, 64, 64)]
        + [rows(128), rows(48), links, links, pltpu.VMEM((4, 32, 128), F32)]
        + [rows(128, I32), rows(128), pltpu.VMEM((2, 32, 128), F32)]
        + [pltpu.VMEM((128, 12, 128), F32)] * 2
        + [dma((8,)), dma((2,)), dma((8,)), dma((8,)), pltpu.SemaphoreType.REGULAR, dma, dma((n // GROUP,))],
        compiler_params=pltpu.CompilerParams(
            collective_id=1, has_side_effects=True, vmem_limit_bytes=VMEM_MB << 20
        ),
    )(temp, salt, east, north, vdiff, kmt, owner, cell, weight)


def hand_kernel(t_in, s_in, atmo_in, t_out, s_out, atmo_out, t_ref, s_ref, atmo_ref, in_sem, out_sem):
    parts = [(atmo_in, atmo_ref, atmo_out)]
    for src, mid, dst in ((t_in, t_ref, t_out), (s_in, s_ref, s_out)):
        for i in range(4):
            rows = slice(16 * i, 16 * i + 16)
            parts.append((src.at[rows], mid.at[rows], dst.at[rows]))
    gets = [pltpu.make_async_copy(p[0], p[1], in_sem.at[i]) for i, p in enumerate(parts)]
    puts = [pltpu.make_async_copy(p[1], p[2], out_sem.at[i]) for i, p in enumerate(parts)]
    for get in gets:
        get.start()
    for get, put in zip(gets, puts):
        get.wait()
        put.start()
    for put in puts:
        put.wait()


def hand_call(temp, salt, atmo):
    hbm = pl.BlockSpec(memory_space=pl.ANY)
    shapes = [jax.ShapeDtypeStruct(a.shape, a.dtype) for a in (temp, salt, atmo)]
    return pl.pallas_call(
        hand_kernel,
        out_shape=tuple(shapes),
        in_specs=[hbm] * 3,
        out_specs=(hbm,) * 3,
        scratch_shapes=[pltpu.VMEM(a.shape, a.dtype) for a in shapes]
        + [pltpu.SemaphoreType.DMA((9,))] * 2,
        compiler_params=pltpu.CompilerParams(vmem_limit_bytes=HAND_MB << 20),
    )(temp, salt, atmo)


def solution(mesh):
    n_lat, n_lon = mesh.shape["lat"], mesh.shape["lon"]
    level, flat = P(None, "lat", "lon"), P("lat", "lon")
    return jax.shard_map(
        lambda *a: hand_call(*whole_call(n_lat, n_lon, *a)),
        mesh=mesh,
        in_specs=(level,) * 5 + (flat,) + (level,) * 3,
        out_specs=(level, level, P(None, ("lat", "lon"))),
        check_vma=False,
    )
```

time: 68.2 us -> 52.7 us (0.77)
  Pallas kernels: 60 us -> 51.8 us
  local copies, waits for them, and re-layouts: 7.08 us -> 0 us
    pallas_call x4 -> x2, Pallas kernels: 60 us -> 51.8 us  [the longest x1 49.3 us: whole_call(): pl.pallas_call(functools.partial(whole_kernel, n_lat, n_lon), out_shape=(...]
    unnamed x15 -> x0, local copies, waits for them, and re-layouts: 7.08 us -> none
where the time goes in v1:
time: 52.7 us; the launch traced here: 52.4 us
  Pallas kernels  51.8 us (98%)
  between operations  0.64 us (1%)
    pallas_call x1, Pallas kernels, whole_call(): pl.pallas_call(functools.partial(whole_kernel, n_lat, n_lon), out_shape=(...  49.3 us
    pallas_call x1, Pallas kernels, hand_call(): pl.pallas_call(hand_kernel, out_shape=tuple(shapes), in_specs=[hbm] * 3,...  2.43 us

profile of v1, /device:TPU:1, one launch (start us, length us, event | category | flops | bytes accessed | tf_op | source)
XLA Modules:
  0.0 52.4 jit_solution(10561738331717156380)
XLA Ops:
  0.6 49.3 %shard_map.112 = (f32[64,32,128]{2,1,0:T(8,128)}, f32[64,32,128]{2,1,0:T(8,128)}, f32[2,2048]{1,0:T(2,128)}) custom-call(f32[64,32,128]{2,1,0:T(8,128)} %temp_hbm.1, f32[64,32,128]{2,1,0:T(8,128)} %salt_hbm.1, f32[64,32,128]{2,1,0:T(8,128)} %east_hbm.1, f32[64,32,128]{2,1,0:T(8,128)} %north_hbm.1, f32[64,32,128]{2,1,0:T(8,128)} %vdiff_hbm.1, ...), custom_call_target="tpu_custom_call" | custom-call | tf_op jit(solution)/shard_map/pallas_call | solution.py:571
  50.0 2.4 %shard_map.113 = (f32[64,32,128]{2,1,0:T(8,128)}, f32[64,32,128]{2,1,0:T(8,128)}, f32[2,2048]{1,0:T(2,128)}) custom-call(f32[64,32,128]{2,1,0:T(8,128)} %get-tuple-element.6.t_in, f32[64,32,128]{2,1,0:T(8,128)} %get-tuple-element.7.s_in, f32[2,2048]{1,0:T(2,128)} %get-tuple-element.8.atmo_in), custom_call_target="tpu_custom_call" | custom-call | tf_op jit(solution)/shard_map/pallas_call | solution.py:611

commit v2 on v1

--- a/solution.py
+++ b/solution.py
@@ -14,8 +14,8 @@
 mixing = 0.1
 GROUP = 16
 FIRST_MERGES = 12
-VMEM_MB = 60
-HAND_MB = 60
+VMEM_MB = 32
+HAND_MB = 8
 
 
 def lanes_of(x, idx):
@@ -180,13 +180,13 @@
 
 def whole_kernel(
     n_lat, n_lon,
-    temp_hbm, salt_hbm, east_hbm, north_hbm, vdiff_hbm, kmt_ref, owner_hbm, cell_hbm, weight_hbm,
-    t_hbm, s_hbm, atmo_ref,
-    t_ref, s_ref, tp, sp, vp, up, vd, inv, gain, back_ref, c_mid, c_east, c_west, c_north, c_south,
+    temp_hbm, salt_hbm, east_hbm, north_hbm, vdiff_hbm, kmt_hbm, owner_hbm, cell_hbm, weight_hbm,
+    t_ref, s_ref, atmo_ref,
+    tp, sp, vp, up, vd, inv, gain, back_ref, c_mid, c_east, c_west, c_north, c_south,
     row_up, row_down, col_out, row_up2, row_down2, col_out2,
     g_north, g_south, g_west, g_east, g_north2, g_south2, g_west2, g_east2,
-    edge, kp, owner_ref, cell_ref, weight_ref, key_ref, load_ref, surf_ref, send, recv,
-    load_sem, store_sem, send_sem, recv_sem, ready, all_send, all_recv,
+    edge, kp, kmt_ref, owner_ref, cell_ref, weight_ref, key_ref, load_ref, surf_ref, send, recv,
+    load_sem, send_sem, recv_sem, ready, all_send, all_recv,
 ):
     n = n_lat * n_lon
     lat, lon = lax.axis_index("lat"), lax.axis_index("lon")
@@ -202,6 +202,7 @@
         pltpu.make_async_copy(src, dst, load_sem.at[i])
         for i, (src, dst) in enumerate(
             (
+                (kmt_hbm, kmt_ref),
                 (temp_hbm, tp.at[:, 8:40, :]),
                 (salt_hbm, sp.at[:, 8:40, :]),
                 (east_hbm, up),
@@ -242,6 +243,7 @@
     lane = lax.broadcasted_iota(I32, (32, 128), 1)
     lane8 = lax.broadcasted_iota(I32, (8, 128), 1)
     sub8 = lax.broadcasted_iota(I32, (8, 128), 0)
+    loads[0].wait()
     kmt = kmt_ref[...].astype(F32)
     kp[8:40, :] = kmt
 
@@ -252,7 +254,7 @@
     def put_rows(value, dst, g, row):
         dst[8 * g : 8 * g + 8, row, :] = value
 
-    for load in loads[:4]:
+    for load in loads[1:5]:
         load.wait()
     for base, src in ((0, tp), (64, sp), (136, vp)):
         take_rows(src, 39, row_up, base)
@@ -269,7 +271,7 @@
         )
 
     zero = jnp.zeros((32, 128), F32)
-    packs = lax.fori_loop(0, 64, pack_level, (zero, zero, zero), unroll=4)
+    packs = lax.fori_loop(0, 64, pack_level, (zero, zero, zero), unroll=16)
     col_out[0:32, :] = packs[0]
     col_out[32:64, :] = packs[1]
     col_out[64:96, :] = at_lane(kmt, 1)
@@ -335,7 +337,7 @@
     start()
     greet_row(ready)
 
-    loads[4].wait()
+    loads[5].wait()
 
     def factor(k, carry):
         above, back = carry
@@ -349,7 +351,7 @@
 
     lax.fori_loop(0, 64, factor, (zero, zero), unroll=4)
 
-    for load in loads[5:]:
+    for load in loads[6:]:
         load.wait()
 
     def hold(keys, loads):
@@ -443,7 +445,7 @@
         c_mid[k], c_east[k], c_west[k], c_north[k], c_south[k] = mid, east, west, north, south
         return advance(k, carry, turn, (mid, east, west, north, south))
 
-    lax.fori_loop(0, 64, down_first, (zero, zero), unroll=2)
+    lax.fori_loop(0, 64, down_first, (zero, zero), unroll=16)
 
     def up_first(i, carry):
         xt, xs, pack_t, pack_s = carry
@@ -458,7 +460,7 @@
         pack_s = jnp.where(pair, at_lane(xs, 2 * k + 1), pack_s)
         return xt, xs, pack_t, pack_s
 
-    _, _, pack_t, pack_s = lax.fori_loop(0, 64, up_first, (zero, zero, zero, zero), unroll=4)
+    _, _, pack_t, pack_s = lax.fori_loop(0, 64, up_first, (zero, zero, zero, zero), unroll=16)
     col_out2[0:32, :] = pack_t
     col_out2[32:64, :] = pack_s
     for base, src in ((0, tp), (64, sp)):
@@ -486,7 +488,7 @@
         turn = lax.rem(128 - 2 * k, 128)
         return advance(k, carry, turn, (c_mid[k], c_east[k], c_west[k], c_north[k], c_south[k]))
 
-    lax.fori_loop(0, 64, down_second, (zero, zero), unroll=2)
+    lax.fori_loop(0, 64, down_second, (zero, zero), unroll=16)
 
     def up_second(i, carry):
         k = 63 - i
@@ -497,13 +499,7 @@
         s_ref[k] = xs
         return xt, xs
 
-    xt, xs = lax.fori_loop(0, 64, up_second, (zero, zero), unroll=4)
-    stores = [
-        pltpu.make_async_copy(t_ref, t_hbm, store_sem.at[0]),
-        pltpu.make_async_copy(s_ref, s_hbm, store_sem.at[1]),
-    ]
-    for store in stores:
-        store.start()
+    xt, xs = lax.fori_loop(0, 64, up_second, (zero, zero), unroll=16)
     wet = jnp.where(kmt > 0.0, 1.0, 0.0)
     surf_ref[0] = xt * wet
     surf_ref[1] = xs * wet
@@ -550,13 +546,11 @@
 
     total = lax.fori_loop(0, n // GROUP, add_group, jnp.zeros((128, 64), F32))
     write_sums(total.T, atmo_ref)
-    for store in stores:
-        store.wait()
     sent = send.at[0 : n - 1]
     pltpu.make_async_copy(sent, sent, all_send).wait()
 
 
-def whole_call(n_lat, n_lon, temp, salt, east, north, vdiff, kmt, owner, cell, weight):
+def whole_call(n_lat, n_lon, *arrays):
     vm = pl.BlockSpec(memory_space=pltpu.VMEM)
     hbm = pl.BlockSpec(memory_space=pltpu.HBM)
     field = jax.ShapeDtypeStruct((64, 32, 128), F32)
@@ -571,35 +565,28 @@
     return pl.pallas_call(
         functools.partial(whole_kernel, n_lat, n_lon),
         out_shape=(field, field, jax.ShapeDtypeStruct((2, 2048), F32)),
-        in_specs=[hbm] * 5 + [vm] + [hbm] * 3,
-        out_specs=(hbm, hbm, vm),
-        scratch_shapes=[block] * 2
-        + [wide] * 3
+        in_specs=[hbm] * 9,
+        out_specs=(vm,) * 3,
+        scratch_shapes=[wide] * 3
         + [block] * 10
         + [rows(r) for r in (200, 136, 128, 128, 128, 64)]
         + [rows(r) for r in (136, 200, 128, 96, 128, 128, 64, 64)]
-        + [rows(128), rows(48), links, links, pltpu.VMEM((4, 32, 128), F32)]
+        + [rows(128), rows(48), pltpu.VMEM((32, 128), I32), links, links, pltpu.VMEM((4, 32, 128), F32)]
         + [rows(128, I32), rows(128), pltpu.VMEM((2, 32, 128), F32)]
         + [pltpu.VMEM((128, 12, 128), F32)] * 2
-        + [dma((8,)), dma((2,)), dma((8,)), dma((8,)), pltpu.SemaphoreType.REGULAR, dma, dma((n // GROUP,))],
+        + [dma((9,)), dma((8,)), dma((8,)), pltpu.SemaphoreType.REGULAR, dma, dma((n // GROUP,))],
         compiler_params=pltpu.CompilerParams(
             collective_id=1, has_side_effects=True, vmem_limit_bytes=VMEM_MB << 20
         ),
-    )(temp, salt, east, north, vdiff, kmt, owner, cell, weight)
-
-
-def hand_kernel(t_in, s_in, atmo_in, t_out, s_out, atmo_out, t_ref, s_ref, atmo_ref, in_sem, out_sem):
-    parts = [(atmo_in, atmo_ref, atmo_out)]
-    for src, mid, dst in ((t_in, t_ref, t_out), (s_in, s_ref, s_out)):
-        for i in range(4):
-            rows = slice(16 * i, 16 * i + 16)
-            parts.append((src.at[rows], mid.at[rows], dst.at[rows]))
-    gets = [pltpu.make_async_copy(p[0], p[1], in_sem.at[i]) for i, p in enumerate(parts)]
-    puts = [pltpu.make_async_copy(p[1], p[2], out_sem.at[i]) for i, p in enumerate(parts)]
-    for get in gets:
-        get.start()
-    for get, put in zip(gets, puts):
-        get.wait()
+    )(*(pltpu.with_memory_space_constraint(a, pltpu.HBM) for a in arrays))
+
+
+def hand_kernel(t_in, s_in, atmo_in, t_out, s_out, atmo_out, sem):
+    puts = [
+        pltpu.make_async_copy(src, dst, sem.at[i])
+        for i, (src, dst) in enumerate(((t_in, t_out), (s_in, s_out), (atmo_in, atmo_out)))
+    ]
+    for put in puts:
         put.start()
     for put in puts:
         put.wait()
@@ -611,10 +598,9 @@
     return pl.pallas_call(
         hand_kernel,
         out_shape=tuple(shapes),
-        in_specs=[hbm] * 3,
+        in_specs=[pl.BlockSpec(memory_space=pltpu.VMEM)] * 3,
         out_specs=(hbm,) * 3,
-        scratch_shapes=[pltpu.VMEM(a.shape, a.dtype) for a in shapes]
-        + [pltpu.SemaphoreType.DMA((9,))] * 2,
+        scratch_shapes=[pltpu.SemaphoreType.DMA((3,))],
         compiler_params=pltpu.CompilerParams(vmem_limit_bytes=HAND_MB << 20),
     )(temp, salt, atmo)
 

time: 52.7 us -> 44.2 us (0.84)
  Pallas kernels: 51.8 us -> 43.4 us
    pallas_call x1, Pallas kernels: 49.3 us -> 42.1 us  [whole_call(): pl.pallas_call(functools.partial(whole_kernel, n_lat, n_lon), out_shape=(...]
    pallas_call x1, Pallas kernels: 2.43 us -> 1.35 us  [hand_call(): pl.pallas_call(hand_kernel, out_shape=tuple(shapes), in_specs=[pl.BlockSp...]
where the time goes in v2:
time: 44.2 us; the launch traced here: 44.1 us
  Pallas kernels  43.4 us (98%)
  between operations  0.64 us (1%)
    pallas_call x1, Pallas kernels, whole_call(): pl.pallas_call(functools.partial(whole_kernel, n_lat, n_lon), out_shape=(...  42.1 us
    pallas_call x1, Pallas kernels, hand_call(): pl.pallas_call(hand_kernel, out_shape=tuple(shapes), in_specs=[pl.BlockSp...  1.35 us

profile of v2, /device:TPU:1, one launch (start us, length us, event | category | flops | bytes accessed | tf_op | source)
XLA Modules:
  0.0 44.1 jit_solution(17211798577583268486)
XLA Ops:
  0.6 42.1 %shard_map.112 = (f32[64,32,128]{2,1,0:T(8,128)S(1)}, f32[64,32,128]{2,1,0:T(8,128)S(1)}, f32[2,2048]{1,0:T(2,128)S(1)}) custom-call(f32[64,32,128]{2,1,0:T(8,128)} %temp_hbm.1, f32[64,32,128]{2,1,0:T(8,128)} %salt_hbm.1, f32[64,32,128]{2,1,0:T(8,128)} %east_hbm.1, f32[64,32,128]{2,1,0:T(8,128)} %north_hbm.1, f32[64,32,128]{2,1,0:T(8,128)} %vdiff_hbm.1, ...), custom_call_target="tpu_custom_call" | custom-call | tf_op jit(solution)/shard_map/pallas_call | solution.py:565
  42.7 1.3 %shard_map.113 = (f32[64,32,128]{2,1,0:T(8,128)}, f32[64,32,128]{2,1,0:T(8,128)}, f32[2,2048]{1,0:T(2,128)}) custom-call(f32[64,32,128]{2,1,0:T(8,128)S(1)} %get-tuple-element.6.t_in, f32[64,32,128]{2,1,0:T(8,128)S(1)} %get-tuple-element.7.s_in, f32[2,2048]{1,0:T(2,128)S(1)} %get-tuple-element.8.atmo_in), custom_call_target="tpu_custom_call" | custom-call | tf_op jit(solution)/shard_map/pallas_call | solution.py:598

commit v3 on v2

--- a/solution.py
+++ b/solution.py
@@ -104,16 +104,15 @@
     return pltpu.roll(x, shift, 1)
 
 
-def group_operands(recv_ref, first):
+def group_operands(recv_ref, cell_ref, first):
     high_id = lax.broadcasted_iota(I32, (16, 128), 0).astype(F32).astype(BF16)
     low_id = lax.broadcasted_iota(I32, (128, 128), 0).astype(F32).astype(BF16)
     left, right = [], []
     for q in range(GROUP):
-        block = recv_ref[first + q]
-        cell = block[8:12]
+        cell = cell_ref[first + q]
         high = jnp.floor(cell * (1.0 / 128.0))
         low = cell - 128.0 * high
-        values = block[0:8]
+        values = recv_ref[first + q]
         coarse = values.astype(BF16).astype(F32)
         fine = values - coarse
         for c in range(4):
@@ -185,8 +184,8 @@
     tp, sp, vp, up, vd, inv, gain, back_ref, c_mid, c_east, c_west, c_north, c_south,
     row_up, row_down, col_out, row_up2, row_down2, col_out2,
     g_north, g_south, g_west, g_east, g_north2, g_south2, g_west2, g_east2,
-    edge, kp, kmt_ref, owner_ref, cell_ref, weight_ref, key_ref, load_ref, surf_ref, send, recv,
-    load_sem, send_sem, recv_sem, ready, all_send, all_recv,
+    edge, kp, kmt_ref, owner_ref, cell_ref, weight_ref, key_ref, load_ref, surf_ref, send, recv, send_cells, recv_cells,
+    load_sem, send_sem, recv_sem, ready, all_send, all_recv, cells_send, cells_recv,
 ):
     n = n_lat * n_lon
     lat, lon = lax.axis_index("lat"), lax.axis_index("lon")
@@ -271,7 +270,7 @@
         )
 
     zero = jnp.zeros((32, 128), F32)
-    packs = lax.fori_loop(0, 64, pack_level, (zero, zero, zero), unroll=16)
+    packs = lax.fori_loop(0, 64, pack_level, (zero, zero, zero), unroll=32)
     col_out[0:32, :] = packs[0]
     col_out[32:64, :] = packs[1]
     col_out[64:96, :] = at_lane(kmt, 1)
@@ -445,7 +444,7 @@
         c_mid[k], c_east[k], c_west[k], c_north[k], c_south[k] = mid, east, west, north, south
         return advance(k, carry, turn, (mid, east, west, north, south))
 
-    lax.fori_loop(0, 64, down_first, (zero, zero), unroll=16)
+    lax.fori_loop(0, 64, down_first, (zero, zero), unroll=32)
 
     def up_first(i, carry):
         xt, xs, pack_t, pack_s = carry
@@ -460,7 +459,7 @@
         pack_s = jnp.where(pair, at_lane(xs, 2 * k + 1), pack_s)
         return xt, xs, pack_t, pack_s
 
-    _, _, pack_t, pack_s = lax.fori_loop(0, 64, up_first, (zero, zero, zero, zero), unroll=16)
+    _, _, pack_t, pack_s = lax.fori_loop(0, 64, up_first, (zero, zero, zero, zero), unroll=32)
     col_out2[0:32, :] = pack_t
     col_out2[32:64, :] = pack_s
     for base, src in ((0, tp), (64, sp)):
@@ -478,7 +477,19 @@
     begin = owner_starts(keys)
     cells = owner_slots([((k >> 12) & 2047).astype(F32) for k in keys], begin)
     for c in range(4):
-        send[:, 8 + c, :] = jnp.concatenate(cells[c], axis=0).T
+        send_cells[:, c, :] = jnp.concatenate(cells[c], axis=0).T
+
+    pl.semaphore_wait(ready, n_lon - 1)
+
+    def send_cell(d):
+        to = lax.rem(me + d, n)
+        pltpu.make_async_remote_copy(
+            src_ref=send_cells.at[to], dst_ref=recv_cells.at[d], send_sem=cells_send,
+            recv_sem=cells_recv,
+            device_id=(to // n_lon, lax.rem(to, n_lon)), device_id_type=MESH,
+        ).start()
+
+    lax.fori_loop(1, n, lambda d, _: (send_cell(d), 0)[1], 0)
 
     finish()
     ghost_rows(g_north2, g_south2, ((0, tp), (64, sp)))
@@ -488,7 +499,7 @@
         turn = lax.rem(128 - 2 * k, 128)
         return advance(k, carry, turn, (c_mid[k], c_east[k], c_west[k], c_north[k], c_south[k]))
 
-    lax.fori_loop(0, 64, down_second, (zero, zero), unroll=16)
+    lax.fori_loop(0, 64, down_second, (zero, zero), unroll=32)
 
     def up_second(i, carry):
         k = 63 - i
@@ -499,7 +510,7 @@
         s_ref[k] = xs
         return xt, xs
 
-    xt, xs = lax.fori_loop(0, 64, up_second, (zero, zero), unroll=16)
+    xt, xs = lax.fori_loop(0, 64, up_second, (zero, zero), unroll=32)
     wet = jnp.where(kmt > 0.0, 1.0, 0.0)
     surf_ref[0] = xt * wet
     surf_ref[1] = xs * wet
@@ -514,8 +525,6 @@
             ]
             send[:, 4 * f + c, :] = jnp.concatenate(kept, axis=0).T
 
-    pl.semaphore_wait(ready, n_lon - 1)
-
     def send_one(d, _):
         to = lax.rem(me + d, n)
         pltpu.make_async_remote_copy(
@@ -527,6 +536,9 @@
 
     lax.fori_loop(1, n, send_one, 0)
     recv[0] = send[me]
+    recv_cells[0] = send_cells[me]
+    got = recv_cells.at[1:n]
+    pltpu.make_async_copy(got, got, cells_recv).wait()
 
     def add_group(g, total):
         @pl.when(g == 0)
@@ -539,7 +551,7 @@
             part = recv.at[pl.ds(pl.multiple_of(g * GROUP, GROUP), GROUP)]
             pltpu.make_async_copy(part, part, all_recv.at[g]).wait()
 
-        left, right = group_operands(recv, g * GROUP)
+        left, right = group_operands(recv, recv_cells, g * GROUP)
         return total + lax.dot_general(
             right, left, (((1,), (1,)), ((), ())), preferred_element_type=F32
         )
@@ -548,6 +560,8 @@
     write_sums(total.T, atmo_ref)
     sent = send.at[0 : n - 1]
     pltpu.make_async_copy(sent, sent, all_send).wait()
+    sent = send_cells.at[0 : n - 1]
+    pltpu.make_async_copy(sent, sent, cells_send).wait()
 
 
 def whole_call(n_lat, n_lon, *arrays):
@@ -573,8 +587,9 @@
         + [rows(r) for r in (136, 200, 128, 96, 128, 128, 64, 64)]
         + [rows(128), rows(48), pltpu.VMEM((32, 128), I32), links, links, pltpu.VMEM((4, 32, 128), F32)]
         + [rows(128, I32), rows(128), pltpu.VMEM((2, 32, 128), F32)]
-        + [pltpu.VMEM((128, 12, 128), F32)] * 2
-        + [dma((9,)), dma((8,)), dma((8,)), pltpu.SemaphoreType.REGULAR, dma, dma((n // GROUP,))],
+        + [pltpu.VMEM((128, 8, 128), F32)] * 2
+        + [pltpu.VMEM((128, 4, 128), F32)] * 2
+        + [dma((9,)), dma((8,)), dma((8,)), pltpu.SemaphoreType.REGULAR, dma, dma((n // GROUP,)), dma, dma],
         compiler_params=pltpu.CompilerParams(
             collective_id=1, has_side_effects=True, vmem_limit_bytes=VMEM_MB << 20
         ),

time: 44.2 us -> 43.3 us (0.980)
  Pallas kernels: 43.4 us -> 42.5 us
    pallas_call x1, Pallas kernels: 42.1 us -> 41.1 us  [whole_call(): pl.pallas_call(functools.partial(whole_kernel, n_lat, n_lon), out_shape=(...]
where the time goes in v3:
time: 43.3 us; the launch traced here: 43.1 us
  Pallas kernels  42.5 us (98%)
  between operations  0.64 us (1%)
    pallas_call x1, Pallas kernels, whole_call(): pl.pallas_call(functools.partial(whole_kernel, n_lat, n_lon), out_shape=(...  41.1 us
    pallas_call x1, Pallas kernels, hand_call(): pl.pallas_call(hand_kernel, out_shape=tuple(shapes), in_specs=[pl.BlockSp...  1.35 us

profile of v3, /device:TPU:1, one launch (start us, length us, event | category | flops | bytes accessed | tf_op | source)
XLA Modules:
  0.0 43.1 jit_solution(13924129215579877767)
XLA Ops:
  0.6 41.1 %shard_map.112 = (f32[64,32,128]{2,1,0:T(8,128)S(1)}, f32[64,32,128]{2,1,0:T(8,128)S(1)}, f32[2,2048]{1,0:T(2,128)S(1)}) custom-call(f32[64,32,128]{2,1,0:T(8,128)} %temp_hbm.1, f32[64,32,128]{2,1,0:T(8,128)} %salt_hbm.1, f32[64,32,128]{2,1,0:T(8,128)} %east_hbm.1, f32[64,32,128]{2,1,0:T(8,128)} %north_hbm.1, f32[64,32,128]{2,1,0:T(8,128)} %vdiff_hbm.1, ...), custom_call_target="tpu_custom_call" | custom-call | tf_op jit(solution)/shard_map/pallas_call | solution.py:579
  41.8 1.3 %shard_map.113 = (f32[64,32,128]{2,1,0:T(8,128)}, f32[64,32,128]{2,1,0:T(8,128)}, f32[2,2048]{1,0:T(2,128)}) custom-call(f32[64,32,128]{2,1,0:T(8,128)S(1)} %get-tuple-element.6.t_in, f32[64,32,128]{2,1,0:T(8,128)S(1)} %get-tuple-element.7.s_in, f32[2,2048]{1,0:T(2,128)S(1)} %get-tuple-element.8.atmo_in), custom_call_target="tpu_custom_call" | custom-call | tf_op jit(solution)/shard_map/pallas_call | solution.py:613

commit v4 on v3

--- a/solution.py
+++ b/solution.py
@@ -271,9 +271,17 @@
 
     zero = jnp.zeros((32, 128), F32)
     packs = lax.fori_loop(0, 64, pack_level, (zero, zero, zero), unroll=32)
-    col_out[0:32, :] = packs[0]
-    col_out[32:64, :] = packs[1]
-    col_out[64:96, :] = at_lane(kmt, 1)
+    odd = (lane & 1) == 1
+
+    def to_west_cols(pack_t, pack_s):
+        return jnp.where(odd, pack_t, at_lane(pack_s, 127))
+
+    def to_east_cols(pack_t, pack_s):
+        return jnp.where(odd, at_lane(pack_s, 1), pack_t)
+
+    col_out[0:32, :] = to_west_cols(packs[0], packs[1])
+    col_out[32:64, :] = at_lane(kmt, 1)
+    col_out[64:96, :] = to_east_cols(packs[0], packs[1])
     col_out[96:128, :] = packs[2]
 
     pl.semaphore_wait(barrier, n_lat + n_lon - 2)
@@ -291,7 +299,7 @@
         to_north = copy(row_n.at[0:up_rows], south.at[0:up_rows], 0, 1, north_id)
         over_fold = copy(row_n.at[0:top_rows], north.at[0:top_rows], 0, 0, north_id)
         to_south = copy(row_s.at[0:down_rows], north.at[0:down_rows], 1, 0, south_id)
-        to_east = copy(col.at[0:east_rows], west.at[0:east_rows], 2, 2, east_id)
+        to_east = copy(col.at[32:east_rows], west.at[32:east_rows], 2, 2, east_id)
         to_west = copy(col.at[0:west_rows], east.at[0:west_rows], 3, 3, west_id)
 
         def start():
@@ -331,7 +339,7 @@
         return start, finish
 
     start, finish = exchange(
-        0, 200, 136, 136, 128, 96, (row_up, row_down, col_out), (g_north, g_south, g_west, g_east)
+        0, 200, 136, 136, 128, 64, (row_up, row_down, col_out), (g_north, g_south, g_west, g_east)
     )
     start()
     greet_row(ready)
@@ -348,7 +356,7 @@
         back_ref[k] = back
         return below, back
 
-    lax.fori_loop(0, 64, factor, (zero, zero), unroll=4)
+    lax.fori_loop(0, 64, factor, (zero, zero), unroll=16)
 
     for load in loads[6:]:
         load.wait()
@@ -381,19 +389,17 @@
                 put_rows(lanes_of(north[rows, :], mirror), dst, g, 40)
                 put_rows(south[rows, :], dst, g, 7)
 
-    def ghost_cols(west, east, count):
-        for i in range(count):
-            rows = slice(32 * i, 32 * i + 32)
-            edge[rows, :] = jnp.where(
-                (lane & 1) == 0, west[rows, :], at_lane(east[rows, :], 126)
-            )
+    def ghost_cols(from_west, from_east):
+        edge[0:32, :] = jnp.where(odd, at_lane(from_east, 126), from_west)
+        edge[32:64, :] = at_lane(jnp.where(odd, from_west, from_east), 127)
 
     ghost_rows(g_north, g_south, ((0, tp), (64, sp)))
     for g in range(8):
         put_rows(g_south[136 + 8 * g : 144 + 8 * g, :], vp, g, 7)
     kp[40:48, :] = lanes_of(g_north[128:136, :], mirror)
     kp[0:8, :] = g_south[128:136, :]
-    ghost_cols(g_west, g_east, 3)
+    ghost_cols(g_west[64:96, :], g_east[0:32, :])
+    edge[64:96, :] = jnp.where(odd, at_lane(g_east[32:64, :], 126), g_west[32:64, :])
     edge[96:128, :] = g_west[96:128, :]
 
     first, last = lane == 0, lane == 127
@@ -460,14 +466,14 @@
         return xt, xs, pack_t, pack_s
 
     _, _, pack_t, pack_s = lax.fori_loop(0, 64, up_first, (zero, zero, zero, zero), unroll=32)
-    col_out2[0:32, :] = pack_t
-    col_out2[32:64, :] = pack_s
+    col_out2[0:32, :] = to_west_cols(pack_t, pack_s)
+    col_out2[32:64, :] = to_east_cols(pack_t, pack_s)
     for base, src in ((0, tp), (64, sp)):
         take_rows(src, 39, row_up2, base)
         take_rows(src, 8, row_down2, base)
 
     start, finish = exchange(
-        4, 128, 128, 128, 64, 64,
+        4, 128, 128, 128, 64, 32,
         (row_up2, row_down2, col_out2), (g_north2, g_south2, g_west2, g_east2),
     )
     start()
@@ -493,7 +499,7 @@
 
     finish()
     ghost_rows(g_north2, g_south2, ((0, tp), (64, sp)))
-    ghost_cols(g_west2, g_east2, 2)
+    ghost_cols(g_west2[32:64, :], g_east2[0:32, :])
 
     def down_second(k, carry):
         turn = lax.rem(128 - 2 * k, 128)
@@ -584,7 +590,7 @@
         scratch_shapes=[wide] * 3
         + [block] * 10
         + [rows(r) for r in (200, 136, 128, 128, 128, 64)]
-        + [rows(r) for r in (136, 200, 128, 96, 128, 128, 64, 64)]
+        + [rows(r) for r in (136, 200, 128, 64, 128, 128, 64, 32)]
         + [rows(128), rows(48), pltpu.VMEM((32, 128), I32), links, links, pltpu.VMEM((4, 32, 128), F32)]
         + [rows(128, I32), rows(128), pltpu.VMEM((2, 32, 128), F32)]
         + [pltpu.VMEM((128, 8, 128), F32)] * 2

time: 43.3 us -> 42.1 us (0.972)
  Pallas kernels: 42.5 us -> 41.3 us
    pallas_call x1, Pallas kernels: 41.1 us -> 39.9 us  [whole_call(): pl.pallas_call(functools.partial(whole_kernel, n_lat, n_lon), out_shape=(...]
where the time goes in v4:
time: 42.1 us; the launch traced here: 41.9 us
  Pallas kernels  41.3 us (98%)
  between operations  0.64 us (2%)
    pallas_call x1, Pallas kernels, whole_call(): pl.pallas_call(functools.partial(whole_kernel, n_lat, n_lon), out_shape=(...  39.9 us
    pallas_call x1, Pallas kernels, hand_call(): pl.pallas_call(hand_kernel, out_shape=tuple(shapes), in_specs=[pl.BlockSp...  1.35 us

profile of v4, /device:TPU:1, one launch (start us, length us, event | category | flops | bytes accessed | tf_op | source)
XLA Modules:
  0.0 41.9 jit_solution(9380366904857808411)
XLA Ops:
  0.6 39.9 %shard_map.112 = (f32[64,32,128]{2,1,0:T(8,128)S(1)}, f32[64,32,128]{2,1,0:T(8,128)S(1)}, f32[2,2048]{1,0:T(2,128)S(1)}) custom-call(f32[64,32,128]{2,1,0:T(8,128)} %temp_hbm.1, f32[64,32,128]{2,1,0:T(8,128)} %salt_hbm.1, f32[64,32,128]{2,1,0:T(8,128)} %east_hbm.1, f32[64,32,128]{2,1,0:T(8,128)} %north_hbm.1, f32[64,32,128]{2,1,0:T(8,128)} %vdiff_hbm.1, ...), custom_call_target="tpu_custom_call" | custom-call | tf_op jit(solution)/shard_map/pallas_call | solution.py:585
  40.6 1.3 %shard_map.113 = (f32[64,32,128]{2,1,0:T(8,128)}, f32[64,32,128]{2,1,0:T(8,128)}, f32[2,2048]{1,0:T(2,128)}) custom-call(f32[64,32,128]{2,1,0:T(8,128)S(1)} %get-tuple-element.6.t_in, f32[64,32,128]{2,1,0:T(8,128)S(1)} %get-tuple-element.7.s_in, f32[2,2048]{1,0:T(2,128)S(1)} %get-tuple-element.8.atmo_in), custom_call_target="tpu_custom_call" | custom-call | tf_op jit(solution)/shard_map/pallas_call | solution.py:619

commit v5 on v4

--- a/solution.py
+++ b/solution.py
@@ -13,7 +13,7 @@
 MESH = pl.DeviceIdType.MESH
 mixing = 0.1
 GROUP = 16
-FIRST_MERGES = 12
+FIRST_MERGES = 13
 VMEM_MB = 32
 HAND_MB = 8
 
@@ -302,7 +302,7 @@
         to_east = copy(col.at[32:east_rows], west.at[32:east_rows], 2, 2, east_id)
         to_west = copy(col.at[0:west_rows], east.at[0:west_rows], 3, 3, west_id)
 
-        def start():
+        def start_rows():
             @pl.when(is_top)
             def _():
                 over_fold.start()
@@ -315,6 +315,7 @@
             def _():
                 to_south.start()
 
+        def start_cols():
             to_east.start()
             to_west.start()
 
@@ -336,12 +337,13 @@
             to_east.wait()
             to_west.wait()
 
-        return start, finish
-
-    start, finish = exchange(
+        return start_rows, start_cols, finish
+
+    start_rows, start_cols, finish = exchange(
         0, 200, 136, 136, 128, 64, (row_up, row_down, col_out), (g_north, g_south, g_west, g_east)
     )
-    start()
+    start_rows()
+    start_cols()
     greet_row(ready)
 
     loads[5].wait()
@@ -466,17 +468,18 @@
         return xt, xs, pack_t, pack_s
 
     _, _, pack_t, pack_s = lax.fori_loop(0, 64, up_first, (zero, zero, zero, zero), unroll=32)
-    col_out2[0:32, :] = to_west_cols(pack_t, pack_s)
-    col_out2[32:64, :] = to_east_cols(pack_t, pack_s)
     for base, src in ((0, tp), (64, sp)):
         take_rows(src, 39, row_up2, base)
         take_rows(src, 8, row_down2, base)
 
-    start, finish = exchange(
+    start_rows, start_cols, finish = exchange(
         4, 128, 128, 128, 64, 32,
         (row_up2, row_down2, col_out2), (g_north2, g_south2, g_west2, g_east2),
     )
-    start()
+    start_rows()
+    col_out2[0:32, :] = to_west_cols(pack_t, pack_s)
+    col_out2[32:64, :] = to_east_cols(pack_t, pack_s)
+    start_cols()
 
     keys, shares = merges(held(key_ref), held(load_ref), range(FIRST_MERGES + 1, 15))
     hold(keys, shares)

time: 42.1 us -> 42.3 us (level)
  no operation moved by 1% of the time
where the time goes in v5:
time: 42.3 us; the launch traced here: 42.1 us
  Pallas kernels  41.5 us (98%)
  between operations  0.64 us (2%)
    pallas_call x1, Pallas kernels, whole_call(): pl.pallas_call(functools.partial(whole_kernel, n_lat, n_lon), out_shape=(...  40.1 us
    pallas_call x1, Pallas kernels, hand_call(): pl.pallas_call(hand_kernel, out_shape=tuple(shapes), in_specs=[pl.BlockSp...  1.35 us

profile of v5, /device:TPU:1, one launch (start us, length us, event | category | flops | bytes accessed | tf_op | source)
XLA Modules:
  0.0 42.1 jit_solution(8162015013933379682)
XLA Ops:
  0.6 40.1 %shard_map.112 = (f32[64,32,128]{2,1,0:T(8,128)S(1)}, f32[64,32,128]{2,1,0:T(8,128)S(1)}, f32[2,2048]{1,0:T(2,128)S(1)}) custom-call(f32[64,32,128]{2,1,0:T(8,128)} %temp_hbm.1, f32[64,32,128]{2,1,0:T(8,128)} %salt_hbm.1, f32[64,32,128]{2,1,0:T(8,128)} %east_hbm.1, f32[64,32,128]{2,1,0:T(8,128)} %north_hbm.1, f32[64,32,128]{2,1,0:T(8,128)} %vdiff_hbm.1, ...), custom_call_target="tpu_custom_call" | custom-call | tf_op jit(solution)/shard_map/pallas_call | solution.py:588
  40.8 1.3 %shard_map.113 = (f32[64,32,128]{2,1,0:T(8,128)}, f32[64,32,128]{2,1,0:T(8,128)}, f32[2,2048]{1,0:T(2,128)}) custom-call(f32[64,32,128]{2,1,0:T(8,128)S(1)} %get-tuple-element.6.t_in, f32[64,32,128]{2,1,0:T(8,128)S(1)} %get-tuple-element.7.s_in, f32[2,2048]{1,0:T(2,128)S(1)} %get-tuple-element.8.atmo_in), custom_call_target="tpu_custom_call" | custom-call | tf_op jit(solution)/shard_map/pallas_call | solution.py:622
